TPU v7x, 128 devices: a whole 4x4x4 slice. The times are simulated.
128 devices in a mesh: rad: 8 (over y_hi, z), ang: 16 (over x, y_lo, core).
Axes of the slice: x: 4, y: 4 (y_hi: 2, y_lo: 2; y = y_hi * 2 + y_lo), z: 4, core: 2. Of those that a mesh axis runs over, the one named last changes fastest.
Arguments:
- coarse_field: float32 [2, 8, 64, 128], P(None, 'rad', 'ang'), may hold values from -6 to 6
- excite_mid: float32 [2, 8, 8, 64, 128], P(None, None, 'rad', 'ang'), may hold values from -6 to 6
- excite_fine: float32 [2, 8, 16, 128, 256], P(None, None, 'rad', 'ang'), may hold values from -6 to 6
- kernels_mid: float32 [16, 8, 27], replicated, may hold values from -0.875 to 0.875
- noise_mid: float32 [16, 8, 8], replicated, may hold values from -1 to 1
- rows_mid: int32 [8], replicated, may hold values from 0 to 15
- kernels_fine: float32 [16, 8, 27], replicated, may hold values from -0.875 to 0.875
- noise_fine: float32 [16, 8, 8], replicated, may hold values from -1 to 1
- rows_fine: int32 [16], replicated, may hold values from 0 to 15
- emission: float32 [32, 256, 512], P('rad', 'ang'), may hold values from 0.3 to 3
- star_bins: int32 [4, 256, 512], P(None, 'ang'), may hold values from 0 to 31
- star_data: float32 [4, 256, 512], P(None, 'ang'), may hold values from -3 to 3
Outputs:
- grad_coarse: float32 [2, 8, 64, 128], P(None, 'rad', 'ang')
- grad_excite_mid: float32 [2, 8, 8, 64, 128], P(None, None, 'rad', 'ang')
- grad_excite_fine: float32 [2, 8, 16, 128, 256], P(None, None, 'rad', 'ang')
- residual: float32 [2, 4, 256, 512], P(None, None, 'ang')
All inputs are finite; a program needn't handle non-finite values.
Results may differ from a plain program's by a relative error of at most 0.0003.
Values sent between devices are 32-bit elements; how exact they have to be, the bound alone decides.
A program may use at most 192 MiB of HBM per device.

v0:
```python
import functools

import jax
import jax.numpy as jnp
from jax import lax
from jax.experimental import pallas as pl
from jax.experimental.pallas import tpu as pltpu
from jax.sharding import PartitionSpec as P

F32 = jnp.float32
BF16 = jnp.bfloat16
MESH = pl.DeviceIdType.MESH
ANY = pl.BlockSpec(memory_space=pl.ANY)
VMEM = pl.BlockSpec(memory_space=pltpu.VMEM)


def lane_shift(x, step):
    if step == 1:
        return x
    width = x.shape[1]
    lane = lax.broadcasted_iota(jnp.int32, x.shape, 1)
    if step == 0:
        return jnp.where(lane == 0, F32(0.0), pltpu.roll(x, 1, 1))
    return jnp.where(lane == width - 1, F32(0.0), pltpu.roll(x, width - 1, 1))


def permuted(x, permutation):
    high = x.astype(BF16)
    rest = x - high.astype(F32)
    mid = rest.astype(BF16)
    low = (rest - mid.astype(F32)).astype(BF16)

    def times(part):
        return jnp.dot(part, permutation, preferred_element_type=F32)

    return times(high) + times(mid) + times(low)


SCRATCH = dict(
    cf_v=pltpu.VMEM((2, 4, 128), F32),
    exm_v=pltpu.VMEM((2, 8, 4, 128), F32),
    exf_v=pltpu.VMEM((2, 8, 2, 8, 256), F32),
    em_v=pltpu.VMEM((4, 64, 128), F32),
    bins_v=pltpu.VMEM((4, 64, 128), jnp.int32),
    data_v=pltpu.VMEM((4, 64, 128), F32),
    km_v=pltpu.VMEM((16, 8, 27), F32),
    nm_v=pltpu.VMEM((8, 8, 16), F32),
    kf_v=pltpu.VMEM((16, 8, 27), F32),
    nf_v=pltpu.VMEM((8, 8, 16), F32),
    rm_s=pltpu.SMEM((8,), jnp.int32),
    rf_s=pltpu.SMEM((16,), jnp.int32),
    spread_m=pltpu.VMEM((256, 256), BF16),
    gather_m=pltpu.VMEM((256, 256), BF16),
    table=pltpu.VMEM((3, 64, 128), F32),
    kern=pltpu.VMEM((3, 8, 27, 8, 128), F32),
    noise=pltpu.VMEM((3, 8, 8, 8, 128), F32),
    csend=pltpu.VMEM((8, 128), F32),
    crecv=pltpu.VMEM((3, 64, 128), F32),
    nsend=pltpu.VMEM((64, 128), F32),
    nrecv=pltpu.VMEM((256, 128), F32),
    nside=pltpu.VMEM((128, 128), F32),
    xsend=pltpu.VMEM((512, 128), F32),
    xrecv=pltpu.VMEM((512, 128), F32),
    esend=pltpu.VMEM((256, 128), F32),
    erecv=pltpu.VMEM((256, 128), F32),
    c12=pltpu.VMEM((12, 16, 128), F32),
    emx=pltpu.VMEM((4, 8, 16, 128), F32),
    cs=pltpu.VMEM((4, 9, 16, 128), F32),
    xi=pltpu.VMEM((4, 2, 16, 256), F32),
    m4=pltpu.VMEM((4, 2, 16, 256), F32),
    fs=pltpu.VMEM((4, 9, 16, 256), F32),
    dv=pltpu.VMEM((4, 4, 16, 256), F32),
    star_x=pltpu.VMEM((2, 8, 8, 512), F32),
    star_y=pltpu.VMEM((2, 4, 8, 128), F32),
    star_z=pltpu.VMEM((2, 2, 16, 128), F32),
    res_x=pltpu.VMEM((2, 32, 128), F32),
    rsend=pltpu.VMEM((64, 128), F32),
    rrecv=pltpu.VMEM((512, 128), F32),
    ws=pltpu.VMEM((4, 9, 16, 256), F32),
    h4=pltpu.VMEM((4, 2, 16, 256), F32),
    wq=pltpu.VMEM((4, 9, 16, 128), F32),
    g12=pltpu.VMEM((12, 16, 128), F32),
    gfsend=pltpu.VMEM((512, 128), F32),
    gfrecv=pltpu.VMEM((512, 128), F32),
    hsend=pltpu.VMEM((320, 128), F32),
    hrecv=pltpu.VMEM((320, 128), F32),
    hedge=pltpu.VMEM((2, 64, 128), F32),
    hside=pltpu.VMEM((2, 16, 128), F32),
    gside=pltpu.VMEM((6, 8, 128), F32),
    gm_x=pltpu.VMEM((64, 128), F32),
    table_sem=pltpu.SemaphoreType.DMA((6,)),
    local_sem=pltpu.SemaphoreType.DMA((15,)),
    self_sem=pltpu.SemaphoreType.DMA((7,)),
    c_send=pltpu.SemaphoreType.DMA((13,)),
    c_recv=pltpu.SemaphoreType.DMA((15,)),
    n_send=pltpu.SemaphoreType.DMA((9,)),
    n_recv=pltpu.SemaphoreType.DMA((15,)),
    x_send=pltpu.SemaphoreType.DMA((7,)),
    x_recv=pltpu.SemaphoreType.DMA((7,)),
    e_send=pltpu.SemaphoreType.DMA((7,)),
    e_recv=pltpu.SemaphoreType.DMA((7,)),
    r_send=pltpu.SemaphoreType.DMA((7,)),
    r_recv=pltpu.SemaphoreType.DMA((7,)),
    f_send=pltpu.SemaphoreType.DMA((7,)),
    f_recv=pltpu.SemaphoreType.DMA((7,)),
    h_send=pltpu.SemaphoreType.DMA((7,)),
    h_recv=pltpu.SemaphoreType.DMA((7,)),
    hs_send=pltpu.SemaphoreType.DMA((8,)),
    hs_recv=pltpu.SemaphoreType.DMA((2,)),
    gs_send=pltpu.SemaphoreType.DMA((8,)),
    gs_recv=pltpu.SemaphoreType.DMA((6,)),
)
INPUTS = ["cf", "exm", "exf", "km", "nm", "rm", "kf", "nf", "rf", "emi", "bins", "data"]
OUTPUTS = ["gc_v", "gm_v", "gf_v", "res_v"]


class Refs:
    def __init__(self, refs):
        for name, ref in zip(INPUTS + OUTPUTS + list(SCRATCH), refs):
            setattr(self, name, ref)


def wide(x):
    return jnp.concatenate([x, x], axis=0)


def wide4(x):
    x = jnp.concatenate([x, x], axis=1)
    return jnp.concatenate([x, x], axis=0)


def row_shift(x, step):
    if step == 1:
        return x
    parts = []
    for s in range(2):
        part = x[8 * s : 8 * s + 8]
        sub = lax.broadcasted_iota(jnp.int32, part.shape, 0)
        if step == 0:
            part = jnp.where(sub == 0, F32(0.0), pltpu.roll(part, 1, 0))
        else:
            part = jnp.where(sub == 7, F32(0.0), pltpu.roll(part, 7, 0))
        parts.append(part)
    return jnp.concatenate(parts, axis=0)


def sums_before(x):
    sub = lax.broadcasted_iota(jnp.int32, x.shape, 0)
    total = x
    for step in (1, 2, 4):
        total = total + jnp.where(sub < step, F32(0.0), pltpu.roll(total, step, 0))
    return jnp.where(sub == 0, F32(0.0), pltpu.roll(total, 1, 0))


def row_total(x):
    for step in (4, 2, 1):
        x = x + pltpu.roll(x, step, 0)
    return x


def kernel(nr, na, *refs):
    v = Refs(refs)
    i = lax.axis_index("rad")
    k = lax.axis_index("ang")
    half_up = lax.shift_right_logical(i + 1, 1)
    low = half_up - 1
    first = 1 - lax.bitwise_and(i, 1)
    none = F32(0.0)

    def row_at(d):
        return lax.rem(i + d, nr)

    def block_at(dk):
        return lax.rem(k + (dk + na), na)

    def remote(src, dst, send, recv, row, dk):
        return pltpu.make_async_remote_copy(
            src_ref=src,
            dst_ref=dst,
            send_sem=send,
            recv_sem=recv,
            device_id=(row, block_at(dk)),
            device_id_type=MESH,
        )

    def part(ref, index, size):
        return ref.at[pl.ds(pl.multiple_of(index * size, size), size)]

    def scatter(src, dst, send, recv, size):
        return [
            remote(
                part(src, row_at(d), size),
                part(dst, i, size),
                send.at[d - 1],
                recv.at[d - 1],
                row_at(d),
                0,
            )
            for d in range(1, nr)
        ]

    def keep_own(src, dst, size, sem):
        return pltpu.make_async_copy(part(src, i, size), part(dst, i, size), sem)

    barrier = pltpu.get_barrier_semaphore()
    for d in range(1, nr):
        pl.semaphore_signal(barrier, inc=1, device_id=(row_at(d), k), device_id_type=MESH)
    for dk in (-1, 1):
        for d in range(nr):
            pl.semaphore_signal(
                barrier, inc=1, device_id=(d, block_at(dk)), device_id_type=MESH
            )

    loads = [
        pltpu.make_async_copy(v.exm.at[:, :, 0], v.exm_v, v.local_sem.at[0]),
        pltpu.make_async_copy(v.cf.at[:, 0], v.cf_v, v.local_sem.at[1]),
    ]
    for c in range(4):
        lanes = pl.ds(128 * c, 128)
        for t, (src, dst) in enumerate(
            ((v.emi, v.em_v), (v.bins, v.bins_v), (v.data, v.data_v))
        ):
            loads.append(
                pltpu.make_async_copy(
                    src.at[:, :, lanes],
                    dst.at[c].reshape(4, 16, 128),
                    v.local_sem.at[2 + 4 * t + c],
                )
            )
    loads.append(pltpu.make_async_copy(v.exf, v.exf_v, v.local_sem.at[14]))
    tables = [
        pltpu.make_async_copy(src, dst, v.table_sem.at[n])
        for n, (src, dst) in enumerate(
            (
                (v.rm, v.rm_s),
                (v.rf, v.rf_s),
                (v.km, v.km_v),
                (v.nm, v.nm_v),
                (v.kf, v.kf_v),
                (v.nf, v.nf_v),
            )
        )
    ]
    for load in [loads[14]] + loads[:14] + tables:
        load.start()

    row = lax.broadcasted_iota(jnp.int32, (256, 256), 0)
    col = lax.broadcasted_iota(jnp.int32, (256, 256), 1)
    v.gather_m[...] = jnp.where(
        row == 2 * lax.bitwise_and(col, 127) + lax.shift_right_logical(col, 7), F32(1.0), none
    ).astype(BF16)
    v.spread_m[...] = jnp.where(
        col == 2 * lax.bitwise_and(row, 127) + lax.shift_right_logical(row, 7), F32(1.0), none
    ).astype(BF16)

    for load in loads + tables:
        load.wait()
    for r in range(2):
        for j in range(8):
            for s in range(2):
                for h in range(2):
                    at = ((r * 8 + j) * 2 + s) * 2 + h
                    v.xsend[pl.ds(at, 8, stride=64), :] = v.exf_v[
                        s, j, r, :, 128 * h : 128 * h + 128
                    ]
    for s in range(2):
        v.csend[4 * s : 4 * s + 4] = v.cf_v[s]
        for j in range(8):
            v.nsend[pl.ds(8 * s + j, 4, stride=16), :] = v.exm_v[s, j]
    pieces = [
        jnp.concatenate(
            [v.em_v[2 * h + e, pl.ds(16 * rl + ca, 8, stride=2), :] for e in range(2)], axis=1
        )
        for rl in range(4)
        for ca in range(2)
        for h in range(2)
    ]
    pieces = permuted(jnp.concatenate(pieces, axis=0), v.gather_m[...])
    for rl in range(4):
        for ca in range(2):
            for h in range(2):
                n = (rl * 2 + ca) * 2 + h
                for cb in range(2):
                    at = h * 16 + rl * 4 + ca * 2 + cb
                    v.esend[pl.ds(at, 8, stride=32), :] = pieces[
                        8 * n : 8 * n + 8, 128 * cb : 128 * cb + 128
                    ]

    for n in range(4):
        for ca in range(2):
            for c in range(4):
                at = pl.ds(16 * n + ca, 8, stride=2)
                lanes = pl.ds(128 * c, 128)
                v.star_x[0, :, 2 * n + ca, lanes] = v.bins_v[c, at, :].astype(F32)
                v.star_x[1, :, 2 * n + ca, lanes] = v.data_v[c, at, :]
    for kind in range(2):
        x = v.star_x[kind, i]
        y = permuted(jnp.concatenate([x[:, :256], x[:, 256:]], axis=0), v.gather_m[...])
        for h in range(2):
            for cb in range(2):
                v.star_y[kind, 2 * h + cb] = y[8 * h : 8 * h + 8, 128 * cb : 128 * cb + 128]
        for h in range(2):
            for cb in range(2):
                for ca in range(2):
                    v.star_z[kind, h, pl.ds(2 * ca + cb, 4, stride=4), :] = v.star_y[
                        kind, 2 * h + cb, pl.ds(ca, 4, stride=2), :
                    ]

    entry = lax.broadcasted_iota(jnp.int32, (8, 16), 1)
    place = lax.broadcasted_iota(jnp.int32, (8, 16), 0)
    chosen = []
    for x in range(3):
        index = jnp.zeros((8, 16), jnp.int32)
        for cell in range(8):
            if x == 0:
                number = v.rm_s[cell]
                v.table[x, pl.ds(cell, 8, stride=8), 0:27] = v.km_v[number]
            else:
                number = v.rf_s[2 * cell + x - 1]
                v.table[x, pl.ds(cell, 8, stride=8), 0:27] = v.kf_v[number]
            index = jnp.where(place == cell, number, index)
        chosen.append(jnp.where(index == entry, F32(1.0), none).astype(BF16))
    for x in range(3):
        for c in range(8):
            tile = v.table[x, 8 * c : 8 * c + 8]
            for o in range(27):
                v.kern[x, c, o] = jnp.broadcast_to(tile[:, o : o + 1], (8, 128))
        source = (v.nm_v if x == 0 else v.nf_v)[...].reshape(64, 16)
        high = source.astype(BF16)
        rest = source - high.astype(F32)
        mid = rest.astype(BF16)
        least = (rest - mid.astype(F32)).astype(BF16)
        tile = None
        for piece in (high, mid, least):
            term = lax.dot_general(
                chosen[x], piece, (((1,), (1,)), ((), ())), preferred_element_type=F32
            )
            tile = term if tile is None else tile + term
        for c in range(8):
            for j in range(8):
                at = 8 * c + j
                v.noise[x, c, j] = jnp.broadcast_to(tile[:, at : at + 1], (8, 128))

    pl.semaphore_wait(barrier, 3 * nr - 1)

    sends_c = [
        remote(
            v.csend,
            v.crecv.at[1, pl.ds(pl.multiple_of(i * 8, 8), 8)],
            v.c_send.at[d - 1],
            v.c_recv.at[d - 1],
            row_at(d),
            0,
        )
        for d in range(1, nr)
    ]
    for side, dk, rows in ((0, 1, (0, 1, 2)), (2, -1, (5, 6, 7))):
        for n, to in enumerate(rows):
            sends_c.append(
                remote(
                    v.csend,
                    v.crecv.at[side, pl.ds(pl.multiple_of(i * 8, 8), 8)],
                    v.c_send.at[7 + (0 if side == 0 else 3) + n],
                    v.c_recv.at[7 + i],
                    to,
                    dk,
                )
            )

    def start_of(owner):
        return jnp.clip(lax.shift_right_logical(owner + 1, 1) - 1, 0, 2)

    sends_n = [
        remote(
            v.nsend.at[pl.ds(pl.multiple_of(start_of(row_at(d)) * 16, 16), 32)],
            part(v.nrecv, i, 32),
            v.n_send.at[d - 1],
            v.n_recv.at[d - 1],
            row_at(d),
            0,
        )
        for d in range(1, nr)
    ]
    sends_n.append(
        remote(v.nsend.at[48:64], part(v.nside, i, 16), v.n_send.at[7], v.n_recv.at[7 + i], 0, 1)
    )
    sends_n.append(
        remote(v.nsend.at[0:16], part(v.nside, i, 16), v.n_send.at[8], v.n_recv.at[7 + i], 7, -1)
    )
    sends_x = scatter(v.xsend, v.xrecv, v.x_send, v.x_recv, 64)
    sends_e = scatter(v.esend, v.erecv, v.e_send, v.e_recv, 32)
    own = [
        pltpu.make_async_copy(
            v.csend, v.crecv.at[1, pl.ds(pl.multiple_of(i * 8, 8), 8)], v.self_sem.at[0]
        ),
        pltpu.make_async_copy(
            v.nsend.at[pl.ds(pl.multiple_of(start_of(i) * 16, 16), 32)],
            part(v.nrecv, i, 32),
            v.self_sem.at[1],
        ),
        keep_own(v.xsend, v.xrecv, 64, v.self_sem.at[2]),
        keep_own(v.esend, v.erecv, 32, v.self_sem.at[3]),
    ]
    for copy in sends_c + sends_n + sends_x + sends_e + own:
        copy.start()

    def arrived(dst, sem):
        pltpu.make_async_copy(dst, dst, sem).wait()

    for copy in sends_c[:7] + sends_n[:7]:
        copy.wait_recv()
    own[0].wait()
    own[1].wait()

    @pl.when(i <= 2)
    def _():
        for n in range(nr):
            arrived(v.crecv.at[0, pl.ds(8 * n, 8)], v.c_recv.at[7 + n])

    @pl.when(i >= 5)
    def _():
        for n in range(nr):
            arrived(v.crecv.at[2, pl.ds(8 * n, 8)], v.c_recv.at[7 + n])

    @pl.when((i == 0) | (i == 7))
    def _():
        for n in range(nr):
            arrived(v.nside.at[pl.ds(16 * n, 16)], v.n_recv.at[7 + n])

    for side in range(3):
        for a in range(4):
            x = jnp.concatenate(
                [v.crecv[side, pl.ds(4 * s + a, 8, stride=8), :] for s in range(2)], axis=0
            )
            if side == 0:
                x = jnp.where(k > 0, x, none)
            if side == 2:
                x = jnp.where(k < na - 1, x, none)
            v.c12[4 * side + a] = x
    for t in range(4):
        x = v.c12[half_up + 2 + t]
        for dr in range(3):
            moved = row_shift(x, dr)
            for db in range(3):
                v.cs[t, 3 * dr + db] = lane_shift(moved, db)
    for j in range(8):
        for n in range(2):
            v.emx[1 + n, j] = jnp.concatenate(
                [v.nrecv[pl.ds(16 * n + 8 * s + j, 8, stride=32), :] for s in range(2)], axis=0
            )
        x = jnp.concatenate(
            [v.nside[pl.ds(8 * s + j, 8, stride=16), :] for s in range(2)], axis=0
        )
        v.emx[0, j] = x
        v.emx[3, j] = x
    base = jnp.where(i > 0, 1, 0) + jnp.where(i == nr - 1, 1, 0)

    def parent_inside(u):
        a = 4 * k + low + u
        return (a >= 0) & (a < 4 * na)

    for u in range(2):
        for cr in range(2):
            sums = [None] * 4
            for j in range(8):
                x = v.emx[base + u, j]
                for q in range(4):
                    term = wide(v.noise[0, 4 * cr + q, j]) * x
                    sums[q] = term if j == 0 else sums[q] + term
            for o in range(27):
                dr, da, db = o // 9, o // 3 % 3, o % 3
                x = v.cs[u + da, 3 * dr + db]
                for q in range(4):
                    sums[q] = sums[q] + wide(v.kern[0, 4 * cr + q, o]) * x
            for q in range(4):
                lanes = slice(128 * (q % 2), 128 * (q % 2) + 128)
                v.xi[2 * u + q // 2, cr, :, lanes] = jnp.where(parent_inside(u), sums[q], none)
    v.m4[...] = permuted(v.xi[...].reshape(128, 256), v.spread_m[...]).reshape(4, 2, 16, 256)
    for da in range(3):
        even = v.m4[first + da, 0]
        odd = v.m4[first + da, 1]
        for m, x in enumerate((row_shift(odd, 0), even, odd, row_shift(even, 2))):
            for db in range(3):
                v.fs[m, 3 * da + db] = lane_shift(x, db)

    for copy in sends_x:
        copy.wait_recv()
    own[2].wait()
    for r in range(2):
        for half in range(2):
            sums = [None] * 4
            for j in range(8):
                at = (r * 8 + j) * 4
                x = jnp.concatenate(
                    [
                        jnp.concatenate(
                            [v.xrecv[pl.ds(at + 2 * s + h, 8, stride=64), :] for h in range(2)],
                            axis=1,
                        )
                        for s in range(2)
                    ],
                    axis=0,
                )
                for q in range(4):
                    term = wide4(v.noise[1 + r, 4 * half + q, j]) * x
                    sums[q] = term if j == 0 else sums[q] + term
            for o in range(27):
                x = v.fs[r + o // 9, o % 9]
                for q in range(4):
                    sums[q] = sums[q] + wide4(v.kern[1 + r, 4 * half + q, o]) * x
            for q in range(4):
                v.dv[2 * r + half, q] = jnp.exp(sums[q])

    for copy in sends_e:
        copy.wait_recv()
    own[3].wait()
    spacing = F32(1.0 / (4 * nr))
    cell = 4 * lax.broadcasted_iota(jnp.int32, (8, 256), 0)
    cells = [(cell + j).astype(F32) for j in range(4)]

    def star(kind, n, q):
        at = 4 * n + q
        return jnp.concatenate(
            [
                jnp.broadcast_to(v.star_z[kind, h, at : at + 1, :], (8, 128))
                for h in range(2)
            ],
            axis=1,
        )

    for q in range(4):
        bins = [star(0, n, q) for n in range(4)]
        light = [
            spacing
            * jnp.concatenate(
                [v.erecv[pl.ds(16 * h + 4 * j + q, 8, stride=32), :] for h in range(2)], axis=1
            )
            for j in range(4)
        ]
        for s in range(2):
            rows = slice(8 * s, 8 * s + 8)
            dens = [v.dv[j, q, rows] for j in range(4)]
            layer = [spacing * x for x in dens]
            depth = sums_before((layer[0] + layer[1]) + (layer[2] + layer[3]))
            shine = []
            for j in range(4):
                shine.append(light[j] * jnp.exp(-depth))
                depth = depth + layer[j]
            column = sums_before((shine[0] + shine[1]) + (shine[2] + shine[3]))
            columns = []
            for j in range(4):
                column = column + shine[j]
                columns.append(column)
            weights = [None] * 4
            for n in range(4):
                picked = jnp.where(bins[n] == cells[0], columns[0], none)
                for j in range(1, 4):
                    picked = jnp.where(bins[n] == cells[j], columns[j], picked)
                picked = row_total(picked)
                left = star(1, n, q) - picked
                for h in range(2):
                    at = 8 * n + 4 * s + q
                    v.res_x[h, at : at + 1] = left[0:1, 128 * h : 128 * h + 128]
                for j in range(4):
                    term = jnp.where(bins[n] > cells[j], left * (picked - columns[j]), none)
                    weights[j] = term if n == 0 else weights[j] + term
            for j in range(4):
                v.dv[j, q, rows] = -dens[j] * weights[j]

    pieces = [
        jnp.concatenate([v.res_x[h, pl.ds(cb, 16, stride=2), :] for cb in range(2)], axis=1)
        for h in range(2)
    ]
    spread = permuted(jnp.concatenate(pieces, axis=0), v.spread_m[...])
    for h in range(2):
        for e in range(2):
            c = 2 * h + e
            v.rsend[16 * c : 16 * c + 16] = spread[
                16 * h : 16 * h + 16, 128 * e : 128 * e + 128
            ]
    sends_r = [
        remote(
            v.rsend, part(v.rrecv, i, 64), v.r_send.at[d - 1], v.r_recv.at[d - 1], row_at(d), 0
        )
        for d in range(1, nr)
    ]
    own_r = pltpu.make_async_copy(v.rsend, part(v.rrecv, i, 64), v.self_sem.at[4])
    for copy in sends_r:
        copy.start()
    own_r.start()

    for r in range(2):
        grads = [v.dv[2 * r + c // 4, c % 4] for c in range(8)]
        for j in range(8):
            total = wide4(v.noise[1 + r, 0, j]) * grads[0]
            for c in range(1, 8):
                total = total + wide4(v.noise[1 + r, c, j]) * grads[c]
            for s in range(2):
                for h in range(2):
                    at = ((8 * s + j) * 2 + r) * 2 + h
                    v.gfsend[pl.ds(at, 8, stride=64), :] = total[
                        8 * s : 8 * s + 8, 128 * h : 128 * h + 128
                    ]
        for o in range(27):
            total = wide4(v.kern[1 + r, 0, o]) * grads[0]
            for c in range(1, 8):
                total = total + wide4(v.kern[1 + r, c, o]) * grads[c]
            m = r + o // 9
            if r == 1 and m < 3:
                total = total + v.ws[m, o % 9]
            v.ws[m, o % 9] = total
    sends_f = scatter(v.gfsend, v.gfrecv, v.f_send, v.f_recv, 64)
    own_f = keep_own(v.gfsend, v.gfrecv, 64, v.self_sem.at[5])
    for copy in sends_f:
        copy.start()
    own_f.start()

    pieces = []
    for da in range(3):
        moved = []
        for m in range(4):
            total = v.ws[m, 3 * da + 1]
            total = total + lane_shift(v.ws[m, 3 * da], 2)
            total = total + lane_shift(v.ws[m, 3 * da + 2], 0)
            moved.append(total)
        pieces.append(moved[1] + row_shift(moved[3], 0))
        pieces.append(moved[2] + row_shift(moved[0], 2))
    spread = permuted(jnp.concatenate(pieces, axis=0), v.gather_m[...])
    v.h4[...] = jnp.zeros(v.h4.shape, F32)
    for da in range(3):
        u_inside = 4 * k + low + lax.shift_right_logical(first + da, 1)
        keep = (u_inside >= 0) & (u_inside < 4 * na)
        for cr in range(2):
            n = (2 * da + cr) * 16
            v.h4[first + da, cr] = jnp.where(keep, spread[n : n + 16], none)

    for u in range(2):
        children = []
        for c in range(8):
            lanes = slice(128 * (c % 2), 128 * (c % 2) + 128)
            children.append(v.h4[2 * u + c // 2 % 2, c // 4, :, lanes])
        for j in range(8):
            total = wide(v.noise[0, 0, j]) * children[0]
            for c in range(1, 8):
                total = total + wide(v.noise[0, c, j]) * children[c]
            for s in range(2):
                v.hsend[pl.ds(16 * u + 8 * s + j, 8, stride=40), :] = total[8 * s : 8 * s + 8]
        for o in range(27):
            dr, da, db = o // 9, o // 3 % 3, o % 3
            total = wide(v.kern[0, 0, o]) * children[0]
            for c in range(1, 8):
                total = total + wide(v.kern[0, c, o]) * children[c]
            t = u + da
            if u == 1 and t < 3:
                total = total + v.wq[t, 3 * dr + db]
            v.wq[t, 3 * dr + db] = total
    v.g12[...] = jnp.zeros(v.g12.shape, F32)
    for t in range(4):
        sums = []
        for dr in range(3):
            total = v.wq[t, 3 * dr + 1]
            total = total + lane_shift(v.wq[t, 3 * dr], 2)
            total = total + lane_shift(v.wq[t, 3 * dr + 2], 0)
            sums.append(row_shift(total, 2 - dr))
        v.g12[half_up + 2 + t] = sums[0] + sums[1] + sums[2]
    for a in range(4):
        for s in range(2):
            rows = slice(8 * s, 8 * s + 8)
            v.hsend[pl.ds(32 + 4 * s + a, 8, stride=40), :] = v.g12[4 + a, rows]
            for side in range(2):
                outside = (k > 0) if side == 0 else (k < na - 1)
                v.hedge[side, pl.ds(4 * s + a, 8, stride=8), :] = jnp.where(
                    outside, v.g12[8 * side + a, rows], none
                )
    sends_h = scatter(v.hsend, v.hrecv, v.h_send, v.h_recv, 40)
    own_h = keep_own(v.hsend, v.hrecv, 40, v.self_sem.at[6])
    for copy in sends_h:
        copy.start()
    own_h.start()
    edges = []
    for side, dk in ((0, -1), (1, 1)):
        moves = [
            remote(
                v.hedge.at[side, pl.ds(8 * n, 8)],
                v.gside.at[i if side == 0 else i - 2],
                v.gs_send.at[n],
                v.gs_recv.at[i if side == 0 else i - 2],
                n,
                dk,
            )
            for n in range(nr)
        ]
        edges.append((i <= 2 if side == 0 else i >= 5, moves))
        moves = [
            remote(
                v.hsend.at[pl.ds(40 * n + 16 * side, 16)],
                v.hside.at[side],
                v.hs_send.at[n],
                v.hs_recv.at[side],
                n,
                dk,
            )
            for n in range(nr)
        ]
        edges.append((i == 0 if side == 0 else i == nr - 1, moves))
    for condition, moves in edges:

        @pl.when(condition)
        def _():
            for copy in moves:
                copy.start()

    for copy in sends_r:
        copy.wait_recv()
    own_r.wait()
    for c in range(4):
        for n in range(4):
            for s in range(2):
                for ca in range(2):
                    at = 16 * c + n * 4 + s * 2 + ca
                    v.res_v[c, pl.ds((s * 4 + n) * 16 + ca, 8, stride=2), :] = v.rrecv[
                        pl.ds(at, 8, stride=64), :
                    ]
    for copy in sends_f:
        copy.wait_recv()
    own_f.wait()
    for s in range(2):
        for j in range(8):
            for r in range(2):
                for h in range(2):
                    at = ((8 * s + j) * 2 + r) * 2 + h
                    v.gf_v[s, j, r, :, 128 * h : 128 * h + 128] = v.gfrecv[
                        pl.ds(at, 8, stride=64), :
                    ]
    for copy in sends_h:
        copy.wait_recv()
    own_h.wait()
    for n in range(6):
        arrived(v.gside.at[n], v.gs_recv.at[n])
    for n in range(2):
        arrived(v.hside.at[n], v.hs_recv.at[n])

    def owed(owner, u):
        at = 40 * owner + 16 * u
        return v.hrecv[at : at + 16]

    by_row = [
        owed(1, 0) + owed(2, 0) + owed(0, 1) + v.hside[1],
        owed(3, 0) + owed(4, 0) + owed(1, 1) + owed(2, 1),
        owed(5, 0) + owed(6, 0) + owed(3, 1) + owed(4, 1),
        owed(7, 0) + owed(5, 1) + owed(6, 1) + v.hside[0],
    ]
    for a in range(4):
        v.gm_x[pl.ds(a, 16, stride=4), :] = by_row[a]
    for s in range(2):
        for j in range(8):
            at = 4 * (8 * s + j)
            v.gm_v[s, j] = v.gm_x[at : at + 4]
    total = v.gside[0]
    for n in range(1, 6):
        total = total + v.gside[n]
    for owner in range(nr):
        total = total + v.hrecv[40 * owner + 32 : 40 * owner + 40]
    for s in range(2):
        v.gc_v[s] = total[4 * s : 4 * s + 4]

    for copy in sends_c + sends_n + sends_x + sends_e + sends_r + sends_f + sends_h:
        copy.wait_send()
    for condition, moves in edges:

        @pl.when(condition)
        def _():
            for copy in moves:
                copy.wait_send()


def hand_out(gc_v, gm_v, gf_v, res_v, gc_o, gm_o, gf_o, res_o, sem):
    outs = [
        pltpu.make_async_copy(gf_v, gf_o, sem.at[0]),
        pltpu.make_async_copy(gm_v, gm_o.at[:, :, 0], sem.at[1]),
        pltpu.make_async_copy(gc_v, gc_o.at[:, 0], sem.at[2]),
    ]
    for c in range(4):
        outs.append(
            pltpu.make_async_copy(
                res_v.at[c].reshape(2, 4, 16, 128),
                res_o.at[:, :, :, pl.ds(128 * c, 128)],
                sem.at[3 + c],
            )
        )
    for out in outs:
        out.start()
    for out in outs:
        out.wait()


def per_device(*args):
    nr, na = lax.axis_size("rad"), lax.axis_size("ang")
    args = list(args)
    for n in (4, 7):
        args[n] = args[n].transpose(1, 2, 0)
    held = [(2, 4, 128), (2, 8, 4, 128), (2, 8, 2, 8, 256), (4, 128, 128)]
    shapes = [(2, 1, 4, 128), (2, 8, 1, 4, 128), (2, 8, 2, 8, 256), (2, 4, 16, 512)]
    results = pl.pallas_call(
        functools.partial(kernel, nr, na),
        out_shape=[pltpu.VMEM(shape, F32) for shape in held],
        in_specs=[ANY] * 12,
        out_specs=[VMEM] * 4,
        scratch_shapes=list(SCRATCH.values()),
        compiler_params=pltpu.CompilerParams(collective_id=0, has_side_effects=True),
    )(*args)
    return pl.pallas_call(
        hand_out,
        out_shape=[jax.ShapeDtypeStruct(shape, F32) for shape in shapes],
        in_specs=[VMEM] * 4,
        out_specs=[ANY] * 4,
        scratch_shapes=[pltpu.SemaphoreType.DMA((7,))],
        compiler_params=pltpu.CompilerParams(vmem_limit_bytes=4 << 20),
    )(*results)


def solution(mesh):
    placed = (
        P(None, "rad", "ang", None),
        P(None, None, "rad", "ang", None),
        P(None, None, "rad", "ang", None),
        P(),
        P(),
        P(),
        P(),
        P(),
        P(),
        P("rad", "ang", None),
        P(None, "ang", None),
        P(None, "ang", None),
    )
    return jax.shard_map(
        per_device,
        mesh=mesh,
        in_specs=placed,
        out_specs=(
            P(None, "rad", "ang", None),
            P(None, None, "rad", "ang", None),
            P(None, None, "rad", "ang", None),
            P(None, None, "ang", None),
        ),
        check_vma=False,
    )
```

profile of v0, /device:TPU:1, one launch (start us, length us, event | category | flops | bytes accessed | tf_op | source)
XLA Modules:
  0.0 34.1 jit_solution(8388947361584666234)
XLA Ops:
  0.6 32.6 %shard_map.147 = (f32[2,4,128]{2,1,0:T(4,128)S(1)}, f32[2,8,4,128]{3,2,1,0:T(4,128)S(1)}, f32[2,8,2,8,256]{4,3,2,1,0:T(8,128)S(1)}, f32[4,128,128]{2,1,0:T(8,128)S(1)}) custom-call(f32[2,1,4,128]{3,2,1,0:T(4,128)} %refs_0_.1, f32[2,8,1,4,128]{4,3,2,1,0:T(4,128)} %refs_1_.1, f32[2,8,2,8,256]{4,3,2,1,0:T(8,128)} %refs_2_.1, f32[16,8,27]{2,1,0:T(8,128)} %refs_3_.1, ...), custom_call_target="tpu_custom_call" | custom-call | tf_op jit(solution)/shard_map/pallas_call | solution.py:804
  33.3 0.9 %shard_map.148 = (f32[2,1,4,128]{3,2,1,0:T(4,128)}, f32[2,8,1,4,128]{4,3,2,1,0:T(4,128)}, f32[2,8,2,8,256]{4,3,2,1,0:T(8,128)}, f32[2,4,16,512]{3,2,1,0:T(8,128)}) custom-call(f32[2,4,128]{2,1,0:T(4,128)S(1)} %get-tuple-element.8.gc_v, f32[2,8,4,128]{3,2,1,0:T(4,128)S(1)} %get-tuple-element.9.gm_v, f32[2,8,2,8,256]{4,3,2,1,0:T(8,128)S(1)} %get-tuple-element.10.gf_v, ...), custom_call_target="tpu_custom_call" | custom-call | tf_op jit(solution)/shard_map/pallas_call | solution.py:812
where the time goes:
time: 34.3 us; the launch traced here: 34.1 us
  Pallas kernels  33.5 us (98%)
  between operations  0.64 us (2%)
    pallas_call x1, Pallas kernels, per_device(): pl.pallas_call(functools.partial(kernel, nr, na), out_shape=[pltpu.VMEM(s...  32.6 us
    pallas_call x1, Pallas kernels, per_device(): pl.pallas_call(hand_out, out_shape=[jax.ShapeDtypeStruct(shape, F32) for...  0.86 us

commit v1 on v0

--- a/solution.py
+++ b/solution.py
@@ -88,28 +88,12 @@
     hside=pltpu.VMEM((2, 16, 128), F32),
     gside=pltpu.VMEM((6, 8, 128), F32),
     gm_x=pltpu.VMEM((64, 128), F32),
-    table_sem=pltpu.SemaphoreType.DMA((6,)),
-    local_sem=pltpu.SemaphoreType.DMA((15,)),
-    self_sem=pltpu.SemaphoreType.DMA((7,)),
-    c_send=pltpu.SemaphoreType.DMA((13,)),
-    c_recv=pltpu.SemaphoreType.DMA((15,)),
-    n_send=pltpu.SemaphoreType.DMA((9,)),
-    n_recv=pltpu.SemaphoreType.DMA((15,)),
-    x_send=pltpu.SemaphoreType.DMA((7,)),
-    x_recv=pltpu.SemaphoreType.DMA((7,)),
-    e_send=pltpu.SemaphoreType.DMA((7,)),
-    e_recv=pltpu.SemaphoreType.DMA((7,)),
-    r_send=pltpu.SemaphoreType.DMA((7,)),
-    r_recv=pltpu.SemaphoreType.DMA((7,)),
-    f_send=pltpu.SemaphoreType.DMA((7,)),
-    f_recv=pltpu.SemaphoreType.DMA((7,)),
-    h_send=pltpu.SemaphoreType.DMA((7,)),
-    h_recv=pltpu.SemaphoreType.DMA((7,)),
-    hs_send=pltpu.SemaphoreType.DMA((8,)),
-    hs_recv=pltpu.SemaphoreType.DMA((2,)),
-    gs_send=pltpu.SemaphoreType.DMA((8,)),
-    gs_recv=pltpu.SemaphoreType.DMA((6,)),
+    load_sem=pltpu.SemaphoreType.DMA((12,)),
+    send_sem=pltpu.SemaphoreType.DMA((9,)),
+    recv_sem=pltpu.SemaphoreType.DMA((12,)),
 )
+SEND = dict(c=0, n=1, x=2, e=3, r=4, f=5, h=6, gs=7, hs=8)
+RECV = dict(c=0, cs=1, n=2, ns=3, x0=4, x1=5, e=6, r=7, f=8, h=9, gs=10, hs=11)
 INPUTS = ["cf", "exm", "exf", "km", "nm", "rm", "kf", "nf", "rf", "emi", "bins", "data"]
 OUTPUTS = ["gc_v", "gm_v", "gf_v", "res_v"]
 
@@ -173,34 +157,65 @@
     def block_at(dk):
         return lax.rem(k + (dk + na), na)
 
-    def remote(src, dst, send, recv, row, dk):
+    def remote(src, dst, group, arrival, row, dk):
         return pltpu.make_async_remote_copy(
             src_ref=src,
             dst_ref=dst,
-            send_sem=send,
-            recv_sem=recv,
+            send_sem=v.send_sem.at[SEND[group]],
+            recv_sem=v.recv_sem.at[RECV[arrival]],
             device_id=(row, block_at(dk)),
             device_id_type=MESH,
         )
 
+    def sent(like, group):
+        pltpu.make_async_copy(like, like, v.send_sem.at[SEND[group]]).wait()
+
+    def arrived(like, arrival):
+        pltpu.make_async_copy(like, like, v.recv_sem.at[RECV[arrival]]).wait()
+
     def part(ref, index, size):
         return ref.at[pl.ds(pl.multiple_of(index * size, size), size)]
 
-    def scatter(src, dst, send, recv, size):
+    def scatter(src, dst, group, size):
         return [
-            remote(
-                part(src, row_at(d), size),
-                part(dst, i, size),
-                send.at[d - 1],
-                recv.at[d - 1],
-                row_at(d),
-                0,
-            )
+            remote(part(src, row_at(d), size), part(dst, i, size), group, group, row_at(d), 0)
             for d in range(1, nr)
         ]
 
-    def keep_own(src, dst, size, sem):
-        return pltpu.make_async_copy(part(src, i, size), part(dst, i, size), sem)
+    def keep_own(src, dst, size):
+        own = pl.ds(pl.multiple_of(i * size, size), size)
+        dst[own] = src[own]
+
+    loads = [
+        [pltpu.make_async_copy(v.exf, v.exf_v, v.load_sem.at[0])],
+        [pltpu.make_async_copy(v.exm.at[:, :, 0], v.exm_v, v.load_sem.at[1])],
+        [pltpu.make_async_copy(v.cf.at[:, 0], v.cf_v, v.load_sem.at[2])],
+    ]
+    for n, (src, dst) in enumerate(((v.emi, v.em_v), (v.bins, v.bins_v), (v.data, v.data_v))):
+        loads.append(
+            [
+                pltpu.make_async_copy(
+                    src.at[:, :, pl.ds(128 * c, 128)],
+                    dst.at[c].reshape(4, 16, 128),
+                    v.load_sem.at[3 + n],
+                )
+                for c in range(4)
+            ]
+        )
+    for n, (src, dst) in enumerate(
+        (
+            (v.rm, v.rm_s),
+            (v.rf, v.rf_s),
+            (v.km, v.km_v),
+            (v.nm, v.nm_v),
+            (v.kf, v.kf_v),
+            (v.nf, v.nf_v),
+        )
+    ):
+        loads.append([pltpu.make_async_copy(src, dst, v.load_sem.at[6 + n])])
+    for group in loads:
+        for load in group:
+            load.start()
 
     barrier = pltpu.get_barrier_semaphore()
     for d in range(1, nr):
@@ -211,50 +226,8 @@
                 barrier, inc=1, device_id=(d, block_at(dk)), device_id_type=MESH
             )
 
-    loads = [
-        pltpu.make_async_copy(v.exm.at[:, :, 0], v.exm_v, v.local_sem.at[0]),
-        pltpu.make_async_copy(v.cf.at[:, 0], v.cf_v, v.local_sem.at[1]),
-    ]
-    for c in range(4):
-        lanes = pl.ds(128 * c, 128)
-        for t, (src, dst) in enumerate(
-            ((v.emi, v.em_v), (v.bins, v.bins_v), (v.data, v.data_v))
-        ):
-            loads.append(
-                pltpu.make_async_copy(
-                    src.at[:, :, lanes],
-                    dst.at[c].reshape(4, 16, 128),
-                    v.local_sem.at[2 + 4 * t + c],
-                )
-            )
-    loads.append(pltpu.make_async_copy(v.exf, v.exf_v, v.local_sem.at[14]))
-    tables = [
-        pltpu.make_async_copy(src, dst, v.table_sem.at[n])
-        for n, (src, dst) in enumerate(
-            (
-                (v.rm, v.rm_s),
-                (v.rf, v.rf_s),
-                (v.km, v.km_v),
-                (v.nm, v.nm_v),
-                (v.kf, v.kf_v),
-                (v.nf, v.nf_v),
-            )
-        )
-    ]
-    for load in [loads[14]] + loads[:14] + tables:
-        load.start()
-
-    row = lax.broadcasted_iota(jnp.int32, (256, 256), 0)
-    col = lax.broadcasted_iota(jnp.int32, (256, 256), 1)
-    v.gather_m[...] = jnp.where(
-        row == 2 * lax.bitwise_and(col, 127) + lax.shift_right_logical(col, 7), F32(1.0), none
-    ).astype(BF16)
-    v.spread_m[...] = jnp.where(
-        col == 2 * lax.bitwise_and(row, 127) + lax.shift_right_logical(row, 7), F32(1.0), none
-    ).astype(BF16)
-
-    for load in loads + tables:
-        load.wait()
+    for group in loads[:3]:
+        group[0].wait()
     for r in range(2):
         for j in range(8):
             for s in range(2):
@@ -267,6 +240,44 @@
         v.csend[4 * s : 4 * s + 4] = v.cf_v[s]
         for j in range(8):
             v.nsend[pl.ds(8 * s + j, 4, stride=16), :] = v.exm_v[s, j]
+
+    pl.semaphore_wait(barrier, 3 * nr - 1)
+
+    def start_of(owner):
+        return jnp.clip(lax.shift_right_logical(owner + 1, 1) - 1, 0, 2)
+
+    def pair_of(owner):
+        return pl.ds(pl.multiple_of(start_of(owner) * 16, 16), 32)
+
+    own8 = pl.ds(pl.multiple_of(i * 8, 8), 8)
+    sends = [
+        remote(v.csend, v.crecv.at[1, own8], "c", "c", row_at(d), 0) for d in range(1, nr)
+    ]
+    for side, dk, rows in ((0, 1, (0, 1, 2)), (2, -1, (5, 6, 7))):
+        sends += [remote(v.csend, v.crecv.at[side, own8], "c", "cs", to, dk) for to in rows]
+    sends += [
+        remote(v.nsend.at[pair_of(row_at(d))], part(v.nrecv, i, 32), "n", "n", row_at(d), 0)
+        for d in range(1, nr)
+    ]
+    sends.append(remote(v.nsend.at[48:64], part(v.nside, i, 16), "n", "ns", 0, 1))
+    sends.append(remote(v.nsend.at[0:16], part(v.nside, i, 16), "n", "ns", 7, -1))
+    for r in range(2):
+        for d in range(1, nr):
+            src = pl.ds(pl.multiple_of(row_at(d) * 64 + 32 * r, 32), 32)
+            dst = pl.ds(pl.multiple_of(i * 64 + 32 * r, 32), 32)
+            sends.append(
+                remote(v.xsend.at[src], v.xrecv.at[dst], "x", "x0" if r == 0 else "x1", row_at(d), 0)
+            )
+    for copy in sends:
+        copy.start()
+
+    row = lax.broadcasted_iota(jnp.int32, (256, 256), 0)
+    col = lax.broadcasted_iota(jnp.int32, (256, 256), 1)
+    v.gather_m[...] = jnp.where(
+        row == 2 * lax.bitwise_and(col, 127) + lax.shift_right_logical(col, 7), F32(1.0), none
+    ).astype(BF16)
+    for load in loads[3]:
+        load.wait()
     pieces = [
         jnp.concatenate(
             [v.em_v[2 * h + e, pl.ds(16 * rl + ca, 8, stride=2), :] for e in range(2)], axis=1
@@ -286,25 +297,20 @@
                         8 * n : 8 * n + 8, 128 * cb : 128 * cb + 128
                     ]
 
-    for n in range(4):
-        for ca in range(2):
-            for c in range(4):
-                at = pl.ds(16 * n + ca, 8, stride=2)
-                lanes = pl.ds(128 * c, 128)
-                v.star_x[0, :, 2 * n + ca, lanes] = v.bins_v[c, at, :].astype(F32)
-                v.star_x[1, :, 2 * n + ca, lanes] = v.data_v[c, at, :]
-    for kind in range(2):
-        x = v.star_x[kind, i]
-        y = permuted(jnp.concatenate([x[:, :256], x[:, 256:]], axis=0), v.gather_m[...])
-        for h in range(2):
-            for cb in range(2):
-                v.star_y[kind, 2 * h + cb] = y[8 * h : 8 * h + 8, 128 * cb : 128 * cb + 128]
-        for h in range(2):
-            for cb in range(2):
-                for ca in range(2):
-                    v.star_z[kind, h, pl.ds(2 * ca + cb, 4, stride=4), :] = v.star_y[
-                        kind, 2 * h + cb, pl.ds(ca, 4, stride=2), :
-                    ]
+    for copy in scatter(v.esend, v.erecv, "e", 32):
+        copy.start()
+
+    v.spread_m[...] = jnp.where(
+        col == 2 * lax.bitwise_and(row, 127) + lax.shift_right_logical(row, 7), F32(1.0), none
+    ).astype(BF16)
+
+    v.crecv[1, own8] = v.csend[...]
+    v.nrecv[pl.ds(pl.multiple_of(i * 32, 32), 32)] = v.nsend[pair_of(i)]
+    keep_own(v.xsend, v.xrecv, 64)
+    keep_own(v.esend, v.erecv, 32)
+    for group in loads[4:]:
+        for load in group:
+            load.wait()
 
     entry = lax.broadcasted_iota(jnp.int32, (8, 16), 1)
     place = lax.broadcasted_iota(jnp.int32, (8, 16), 0)
@@ -341,91 +347,36 @@
                 at = 8 * c + j
                 v.noise[x, c, j] = jnp.broadcast_to(tile[:, at : at + 1], (8, 128))
 
-    pl.semaphore_wait(barrier, 3 * nr - 1)
-
-    sends_c = [
-        remote(
-            v.csend,
-            v.crecv.at[1, pl.ds(pl.multiple_of(i * 8, 8), 8)],
-            v.c_send.at[d - 1],
-            v.c_recv.at[d - 1],
-            row_at(d),
-            0,
-        )
-        for d in range(1, nr)
-    ]
-    for side, dk, rows in ((0, 1, (0, 1, 2)), (2, -1, (5, 6, 7))):
-        for n, to in enumerate(rows):
-            sends_c.append(
-                remote(
-                    v.csend,
-                    v.crecv.at[side, pl.ds(pl.multiple_of(i * 8, 8), 8)],
-                    v.c_send.at[7 + (0 if side == 0 else 3) + n],
-                    v.c_recv.at[7 + i],
-                    to,
-                    dk,
-                )
-            )
-
-    def start_of(owner):
-        return jnp.clip(lax.shift_right_logical(owner + 1, 1) - 1, 0, 2)
-
-    sends_n = [
-        remote(
-            v.nsend.at[pl.ds(pl.multiple_of(start_of(row_at(d)) * 16, 16), 32)],
-            part(v.nrecv, i, 32),
-            v.n_send.at[d - 1],
-            v.n_recv.at[d - 1],
-            row_at(d),
-            0,
-        )
-        for d in range(1, nr)
-    ]
-    sends_n.append(
-        remote(v.nsend.at[48:64], part(v.nside, i, 16), v.n_send.at[7], v.n_recv.at[7 + i], 0, 1)
-    )
-    sends_n.append(
-        remote(v.nsend.at[0:16], part(v.nside, i, 16), v.n_send.at[8], v.n_recv.at[7 + i], 7, -1)
-    )
-    sends_x = scatter(v.xsend, v.xrecv, v.x_send, v.x_recv, 64)
-    sends_e = scatter(v.esend, v.erecv, v.e_send, v.e_recv, 32)
-    own = [
-        pltpu.make_async_copy(
-            v.csend, v.crecv.at[1, pl.ds(pl.multiple_of(i * 8, 8), 8)], v.self_sem.at[0]
-        ),
-        pltpu.make_async_copy(
-            v.nsend.at[pl.ds(pl.multiple_of(start_of(i) * 16, 16), 32)],
-            part(v.nrecv, i, 32),
-            v.self_sem.at[1],
-        ),
-        keep_own(v.xsend, v.xrecv, 64, v.self_sem.at[2]),
-        keep_own(v.esend, v.erecv, 32, v.self_sem.at[3]),
-    ]
-    for copy in sends_c + sends_n + sends_x + sends_e + own:
-        copy.start()
-
-    def arrived(dst, sem):
-        pltpu.make_async_copy(dst, dst, sem).wait()
-
-    for copy in sends_c[:7] + sends_n[:7]:
-        copy.wait_recv()
-    own[0].wait()
-    own[1].wait()
-
-    @pl.when(i <= 2)
+    for n in range(4):
+        for ca in range(2):
+            for c in range(4):
+                at = pl.ds(16 * n + ca, 8, stride=2)
+                lanes = pl.ds(128 * c, 128)
+                v.star_x[0, :, 2 * n + ca, lanes] = v.bins_v[c, at, :].astype(F32)
+                v.star_x[1, :, 2 * n + ca, lanes] = v.data_v[c, at, :]
+    for kind in range(2):
+        x = v.star_x[kind, i]
+        y = permuted(jnp.concatenate([x[:, :256], x[:, 256:]], axis=0), v.gather_m[...])
+        for h in range(2):
+            for cb in range(2):
+                v.star_y[kind, 2 * h + cb] = y[8 * h : 8 * h + 8, 128 * cb : 128 * cb + 128]
+        for h in range(2):
+            for cb in range(2):
+                for ca in range(2):
+                    v.star_z[kind, h, pl.ds(2 * ca + cb, 4, stride=4), :] = v.star_y[
+                        kind, 2 * h + cb, pl.ds(ca, 4, stride=2), :
+                    ]
+
+    arrived(v.crecv.at[1, 0:56], "c")
+    arrived(v.nrecv.at[0:224], "n")
+
+    @pl.when((i <= 2) | (i >= 5))
     def _():
-        for n in range(nr):
-            arrived(v.crecv.at[0, pl.ds(8 * n, 8)], v.c_recv.at[7 + n])
-
-    @pl.when(i >= 5)
+        arrived(v.crecv.at[0], "cs")
+
+    @pl.when((i == 0) | (i == nr - 1))
     def _():
-        for n in range(nr):
-            arrived(v.crecv.at[2, pl.ds(8 * n, 8)], v.c_recv.at[7 + n])
-
-    @pl.when((i == 0) | (i == 7))
-    def _():
-        for n in range(nr):
-            arrived(v.nside.at[pl.ds(16 * n, 16)], v.n_recv.at[7 + n])
+        arrived(v.nside, "ns")
 
     for side in range(3):
         for a in range(4):
@@ -483,10 +434,8 @@
             for db in range(3):
                 v.fs[m, 3 * da + db] = lane_shift(x, db)
 
-    for copy in sends_x:
-        copy.wait_recv()
-    own[2].wait()
     for r in range(2):
+        arrived(v.xrecv.at[0:224], "x0" if r == 0 else "x1")
         for half in range(2):
             sums = [None] * 4
             for j in range(8):
@@ -511,9 +460,7 @@
             for q in range(4):
                 v.dv[2 * r + half, q] = jnp.exp(sums[q])
 
-    for copy in sends_e:
-        copy.wait_recv()
-    own[3].wait()
+    arrived(v.erecv.at[0:224], "e")
     spacing = F32(1.0 / (4 * nr))
     cell = 4 * lax.broadcasted_iota(jnp.int32, (8, 256), 0)
     cells = [(cell + j).astype(F32) for j in range(4)]
@@ -578,16 +525,9 @@
             v.rsend[16 * c : 16 * c + 16] = spread[
                 16 * h : 16 * h + 16, 128 * e : 128 * e + 128
             ]
-    sends_r = [
-        remote(
-            v.rsend, part(v.rrecv, i, 64), v.r_send.at[d - 1], v.r_recv.at[d - 1], row_at(d), 0
-        )
-        for d in range(1, nr)
-    ]
-    own_r = pltpu.make_async_copy(v.rsend, part(v.rrecv, i, 64), v.self_sem.at[4])
-    for copy in sends_r:
-        copy.start()
-    own_r.start()
+    for d in range(1, nr):
+        remote(v.rsend, part(v.rrecv, i, 64), "r", "r", row_at(d), 0).start()
+    v.rrecv[pl.ds(pl.multiple_of(i * 64, 64), 64)] = v.rsend[...]
 
     for r in range(2):
         grads = [v.dv[2 * r + c // 4, c % 4] for c in range(8)]
@@ -609,11 +549,9 @@
             if r == 1 and m < 3:
                 total = total + v.ws[m, o % 9]
             v.ws[m, o % 9] = total
-    sends_f = scatter(v.gfsend, v.gfrecv, v.f_send, v.f_recv, 64)
-    own_f = keep_own(v.gfsend, v.gfrecv, 64, v.self_sem.at[5])
-    for copy in sends_f:
+    for copy in scatter(v.gfsend, v.gfrecv, "f", 64):
         copy.start()
-    own_f.start()
+    keep_own(v.gfsend, v.gfrecv, 64)
 
     pieces = []
     for da in range(3):
@@ -672,47 +610,27 @@
                 v.hedge[side, pl.ds(4 * s + a, 8, stride=8), :] = jnp.where(
                     outside, v.g12[8 * side + a, rows], none
                 )
-    sends_h = scatter(v.hsend, v.hrecv, v.h_send, v.h_recv, 40)
-    own_h = keep_own(v.hsend, v.hrecv, 40, v.self_sem.at[6])
-    for copy in sends_h:
+    for copy in scatter(v.hsend, v.hrecv, "h", 40):
         copy.start()
-    own_h.start()
-    edges = []
+    keep_own(v.hsend, v.hrecv, 40)
     for side, dk in ((0, -1), (1, 1)):
-        moves = [
-            remote(
-                v.hedge.at[side, pl.ds(8 * n, 8)],
-                v.gside.at[i if side == 0 else i - 2],
-                v.gs_send.at[n],
-                v.gs_recv.at[i if side == 0 else i - 2],
-                n,
-                dk,
-            )
-            for n in range(nr)
-        ]
-        edges.append((i <= 2 if side == 0 else i >= 5, moves))
-        moves = [
-            remote(
-                v.hsend.at[pl.ds(40 * n + 16 * side, 16)],
-                v.hside.at[side],
-                v.hs_send.at[n],
-                v.hs_recv.at[side],
-                n,
-                dk,
-            )
-            for n in range(nr)
-        ]
-        edges.append((i == 0 if side == 0 else i == nr - 1, moves))
-    for condition, moves in edges:
-
-        @pl.when(condition)
+
+        @pl.when(i <= 2 if side == 0 else i >= 5)
         def _():
-            for copy in moves:
-                copy.start()
-
-    for copy in sends_r:
-        copy.wait_recv()
-    own_r.wait()
+            place = i if side == 0 else i - 2
+            for n in range(nr):
+                remote(
+                    v.hedge.at[side, pl.ds(8 * n, 8)], v.gside.at[place], "gs", "gs", n, dk
+                ).start()
+
+        @pl.when(i == 0 if side == 0 else i == nr - 1)
+        def _():
+            for n in range(nr):
+                remote(
+                    v.hsend.at[pl.ds(40 * n + 16 * side, 16)], v.hside.at[side], "hs", "hs", n, dk
+                ).start()
+
+    arrived(v.rrecv.at[0:448], "r")
     for c in range(4):
         for n in range(4):
             for s in range(2):
@@ -721,9 +639,7 @@
                     v.res_v[c, pl.ds((s * 4 + n) * 16 + ca, 8, stride=2), :] = v.rrecv[
                         pl.ds(at, 8, stride=64), :
                     ]
-    for copy in sends_f:
-        copy.wait_recv()
-    own_f.wait()
+    arrived(v.gfrecv.at[0:448], "f")
     for s in range(2):
         for j in range(8):
             for r in range(2):
@@ -732,13 +648,9 @@
                     v.gf_v[s, j, r, :, 128 * h : 128 * h + 128] = v.gfrecv[
                         pl.ds(at, 8, stride=64), :
                     ]
-    for copy in sends_h:
-        copy.wait_recv()
-    own_h.wait()
-    for n in range(6):
-        arrived(v.gside.at[n], v.gs_recv.at[n])
-    for n in range(2):
-        arrived(v.hside.at[n], v.hs_recv.at[n])
+    arrived(v.hrecv.at[0:280], "h")
+    arrived(v.gside, "gs")
+    arrived(v.hside, "hs")
 
     def owed(owner, u):
         at = 40 * owner + 16 * u
@@ -764,14 +676,21 @@
     for s in range(2):
         v.gc_v[s] = total[4 * s : 4 * s + 4]
 
-    for copy in sends_c + sends_n + sends_x + sends_e + sends_r + sends_f + sends_h:
-        copy.wait_send()
-    for condition, moves in edges:
-
-        @pl.when(condition)
-        def _():
-            for copy in moves:
-                copy.wait_send()
+    sent(v.xsend.at[0:104], "c")
+    sent(v.xsend.at[0:256], "n")
+    sent(v.xsend.at[0:448], "x")
+    sent(v.xsend.at[0:224], "e")
+    sent(v.xsend.at[0:448], "r")
+    sent(v.xsend.at[0:448], "f")
+    sent(v.xsend.at[0:280], "h")
+
+    @pl.when((i <= 2) | (i >= 5))
+    def _():
+        sent(v.xsend.at[0:64], "gs")
+
+    @pl.when((i == 0) | (i == nr - 1))
+    def _():
+        sent(v.xsend.at[0:128], "hs")
 
 
 def hand_out(gc_v, gm_v, gf_v, res_v, gc_o, gm_o, gf_o, res_o, sem):

time: 34.3 us -> 32.5 us (0.948)
  the two profiles are of different devices: /device:TPU:1 before, /device:TPU:3 now
where the time goes in v1:
time: 32.5 us; the launch traced here: 32.3 us
  Pallas kernels  31.7 us (98%)
  between operations  0.64 us (2%)
    pallas_call x1, Pallas kernels, per_device(): pl.pallas_call(functools.partial(kernel, nr, na), out_shape=[pltpu.VMEM(s...  30.8 us
    pallas_call x1, Pallas kernels, per_device(): pl.pallas_call(hand_out, out_shape=[jax.ShapeDtypeStruct(shape, F32) for...  0.86 us

profile of v1, /device:TPU:3, one launch (start us, length us, event | category | flops | bytes accessed | tf_op | source)
XLA Modules:
  0.0 32.3 jit_solution(3470559330437278487)
XLA Ops:
  0.6 30.8 %shard_map.147 = (f32[2,4,128]{2,1,0:T(4,128)S(1)}, f32[2,8,4,128]{3,2,1,0:T(4,128)S(1)}, f32[2,8,2,8,256]{4,3,2,1,0:T(8,128)S(1)}, f32[4,128,128]{2,1,0:T(8,128)S(1)}) custom-call(f32[2,1,4,128]{3,2,1,0:T(4,128)} %refs_0_.1, f32[2,8,1,4,128]{4,3,2,1,0:T(4,128)} %refs_1_.1, f32[2,8,2,8,256]{4,3,2,1,0:T(8,128)} %refs_2_.1, f32[16,8,27]{2,1,0:T(8,128)} %refs_3_.1, ...), custom_call_target="tpu_custom_call" | custom-call | tf_op jit(solution)/shard_map/pallas_call | solution.py:723
  31.5 0.9 %shard_map.148 = (f32[2,1,4,128]{3,2,1,0:T(4,128)}, f32[2,8,1,4,128]{4,3,2,1,0:T(4,128)}, f32[2,8,2,8,256]{4,3,2,1,0:T(8,128)}, f32[2,4,16,512]{3,2,1,0:T(8,128)}) custom-call(f32[2,4,128]{2,1,0:T(4,128)S(1)} %get-tuple-element.8.gc_v, f32[2,8,4,128]{3,2,1,0:T(4,128)S(1)} %get-tuple-element.9.gm_v, f32[2,8,2,8,256]{4,3,2,1,0:T(8,128)S(1)} %get-tuple-element.10.gf_v, ...), custom_call_target="tpu_custom_call" | custom-call | tf_op jit(solution)/shard_map/pallas_call | solution.py:731

commit v2 on v1

v2 whole, which is shorter than its diff:
```python
import functools

import jax
import jax.numpy as jnp
from jax import lax
from jax.experimental import pallas as pl
from jax.experimental.pallas import tpu as pltpu
from jax.sharding import PartitionSpec as P

F32 = jnp.float32
BF16 = jnp.bfloat16
MESH = pl.DeviceIdType.MESH
ANY = pl.BlockSpec(memory_space=pl.ANY)
VMEM = pl.BlockSpec(memory_space=pltpu.VMEM)


def lane_shift(x, step):
    if step == 1:
        return x
    width = x.shape[1]
    lane = lax.broadcasted_iota(jnp.int32, x.shape, 1)
    if step == 0:
        return jnp.where(lane == 0, F32(0.0), pltpu.roll(x, 1, 1))
    return jnp.where(lane == width - 1, F32(0.0), pltpu.roll(x, width - 1, 1))


def permuted(x, permutation):
    high = x.astype(BF16)
    rest = x - high.astype(F32)
    mid = rest.astype(BF16)
    low = (rest - mid.astype(F32)).astype(BF16)

    def times(part):
        return jnp.dot(part, permutation, preferred_element_type=F32)

    return times(high) + times(mid) + times(low)


SCRATCH = dict(
    cf_v=pltpu.VMEM((2, 4, 128), F32),
    exm_v=pltpu.VMEM((2, 8, 4, 128), F32),
    exf_v=pltpu.VMEM((2, 8, 2, 8, 256), F32),
    em_v=pltpu.VMEM((4, 64, 128), F32),
    bins_v=pltpu.VMEM((4, 64, 128), jnp.int32),
    data_v=pltpu.VMEM((4, 64, 128), F32),
    km_v=pltpu.VMEM((16, 8, 27), F32),
    nm_v=pltpu.VMEM((8, 8, 16), F32),
    kf_v=pltpu.VMEM((16, 8, 27), F32),
    nf_v=pltpu.VMEM((8, 8, 16), F32),
    rm_s=pltpu.SMEM((8,), jnp.int32),
    rf_s=pltpu.SMEM((16,), jnp.int32),
    spread_m=pltpu.VMEM((256, 256), BF16),
    gather_m=pltpu.VMEM((256, 256), BF16),
    table=pltpu.VMEM((3, 64, 128), F32),
    kern=pltpu.VMEM((3, 8, 27, 8, 128), F32),
    noise=pltpu.VMEM((3, 8, 8, 8, 128), F32),
    csend=pltpu.VMEM((8, 128), F32),
    crecv=pltpu.VMEM((3, 64, 128), F32),
    nsend=pltpu.VMEM((64, 128), F32),
    nrecv=pltpu.VMEM((256, 128), F32),
    nside=pltpu.VMEM((128, 128), F32),
    xsend=pltpu.VMEM((512, 128), F32),
    xrecv=pltpu.VMEM((512, 128), F32),
    esend=pltpu.VMEM((256, 128), F32),
    erecv=pltpu.VMEM((256, 128), F32),
    c12=pltpu.VMEM((12, 2, 8, 128), F32),
    emx=pltpu.VMEM((4, 8, 8, 128), F32),
    cs=pltpu.VMEM((4, 9, 8, 128), F32),
    xi=pltpu.VMEM((4, 2, 8, 256), F32),
    m4=pltpu.VMEM((4, 2, 8, 256), F32),
    fs=pltpu.VMEM((4, 9, 8, 256), F32),
    dv=pltpu.VMEM((4, 4, 8, 256), F32),
    star_x=pltpu.VMEM((2, 8, 8, 512), F32),
    star_y=pltpu.VMEM((2, 4, 8, 128), F32),
    star_z=pltpu.VMEM((2, 2, 16, 128), F32),
    res_x=pltpu.VMEM((2, 16, 128), F32),
    rsend=pltpu.VMEM((64, 128), F32),
    rrecv=pltpu.VMEM((512, 128), F32),
    ws=pltpu.VMEM((4, 9, 8, 256), F32),
    h4=pltpu.VMEM((4, 2, 8, 256), F32),
    wq=pltpu.VMEM((4, 9, 8, 128), F32),
    g12=pltpu.VMEM((12, 8, 128), F32),
    gfsend=pltpu.VMEM((512, 128), F32),
    gfrecv=pltpu.VMEM((512, 128), F32),
    hsend=pltpu.VMEM((320, 128), F32),
    hrecv=pltpu.VMEM((320, 128), F32),
    hedge=pltpu.VMEM((2, 64, 128), F32),
    hside=pltpu.VMEM((2, 2, 8, 128), F32),
    gside=pltpu.VMEM((6, 8, 128), F32),
    gm_x=pltpu.VMEM((64, 128), F32),
    load_sem=pltpu.SemaphoreType.DMA((12,)),
    send_sem=pltpu.SemaphoreType.DMA((9,)),
    recv_sem=pltpu.SemaphoreType.DMA((17,)),
)
SEND = dict(c=0, n=1, x=2, e=3, r=4, f=5, h=6, gs=7, hs=8)
RECV = {
    name: number
    for number, name in enumerate(
        ["c", "cs", "n0", "n1", "ns0", "ns1", "x0", "x1", "e"]
        + ["r0", "r1", "f0", "f1", "h0", "h1", "gs", "hs"]
    )
}
INPUTS = ["cf", "exm", "exf", "km", "nm", "rm", "kf", "nf", "rf", "emi", "bins", "data"]
OUTPUTS = ["gc_v", "gm_v", "gf_v", "res_v"]


class Refs:
    def __init__(self, refs):
        for name, ref in zip(INPUTS + OUTPUTS + list(SCRATCH), refs):
            setattr(self, name, ref)


def wide(x):
    return jnp.concatenate([x, x], axis=1)


def row_shift(x, step):
    if step == 1:
        return x
    sub = lax.broadcasted_iota(jnp.int32, x.shape, 0)
    if step == 0:
        return jnp.where(sub == 0, F32(0.0), pltpu.roll(x, 1, 0))
    return jnp.where(sub == 7, F32(0.0), pltpu.roll(x, 7, 0))


def weighted(weights, values):
    total = weights[0] * values[0]
    for weight, value in zip(weights[1:], values[1:]):
        total = total + weight * value
    return total


def sums_before(x):
    sub = lax.broadcasted_iota(jnp.int32, x.shape, 0)
    total = x
    for step in (1, 2, 4):
        total = total + jnp.where(sub < step, F32(0.0), pltpu.roll(total, step, 0))
    return jnp.where(sub == 0, F32(0.0), pltpu.roll(total, 1, 0))


def row_total(x):
    for step in (4, 2, 1):
        x = x + pltpu.roll(x, step, 0)
    return x


def kernel(nr, na, *refs):
    v = Refs(refs)
    i = lax.axis_index("rad")
    k = lax.axis_index("ang")
    half_up = lax.shift_right_logical(i + 1, 1)
    low = half_up - 1
    first = 1 - lax.bitwise_and(i, 1)
    none = F32(0.0)

    def row_at(d):
        return lax.rem(i + d, nr)

    def block_at(dk):
        return lax.rem(k + (dk + na), na)

    def remote(src, dst, group, arrival, row, dk):
        return pltpu.make_async_remote_copy(
            src_ref=src,
            dst_ref=dst,
            send_sem=v.send_sem.at[SEND[group]],
            recv_sem=v.recv_sem.at[RECV[arrival]],
            device_id=(row, block_at(dk)),
            device_id_type=MESH,
        )

    def sent(like, group):
        pltpu.make_async_copy(like, like, v.send_sem.at[SEND[group]]).wait()

    def arrived(like, arrival):
        pltpu.make_async_copy(like, like, v.recv_sem.at[RECV[arrival]]).wait()

    def part(ref, index, size):
        return ref.at[pl.ds(pl.multiple_of(index * size, size), size)]

    def rows_of(index, size, offset):
        return pl.ds(pl.multiple_of(index * size + offset, 8), size)

    def scatter(src, dst, group, arrival, size, offset=0):
        for d in range(1, nr):
            remote(
                src.at[rows_of(row_at(d), size, offset)],
                dst.at[rows_of(i, size, offset)],
                group,
                arrival,
                row_at(d),
                0,
            ).start()

    def keep_own(src, dst, size, offset=0):
        own = rows_of(i, size, offset)
        dst[own] = src[own]

    loads = [
        [pltpu.make_async_copy(v.exf, v.exf_v, v.load_sem.at[0])],
        [pltpu.make_async_copy(v.exm.at[:, :, 0], v.exm_v, v.load_sem.at[1])],
        [pltpu.make_async_copy(v.cf.at[:, 0], v.cf_v, v.load_sem.at[2])],
    ]
    for n, (src, dst) in enumerate(((v.emi, v.em_v), (v.bins, v.bins_v), (v.data, v.data_v))):
        loads.append(
            [
                pltpu.make_async_copy(
                    src.at[:, :, pl.ds(128 * c, 128)],
                    dst.at[c].reshape(4, 16, 128),
                    v.load_sem.at[3 + n],
                )
                for c in range(4)
            ]
        )
    for n, (src, dst) in enumerate(
        (
            (v.rm, v.rm_s),
            (v.rf, v.rf_s),
            (v.km, v.km_v),
            (v.nm, v.nm_v),
            (v.kf, v.kf_v),
            (v.nf, v.nf_v),
        )
    ):
        loads.append([pltpu.make_async_copy(src, dst, v.load_sem.at[6 + n])])
    for group in loads:
        for load in group:
            load.start()

    barrier = pltpu.get_barrier_semaphore()
    for d in range(1, nr):
        pl.semaphore_signal(barrier, inc=1, device_id=(row_at(d), k), device_id_type=MESH)
    for dk in (-1, 1):
        for d in range(nr):
            pl.semaphore_signal(
                barrier, inc=1, device_id=(d, block_at(dk)), device_id_type=MESH
            )

    for group in loads[:3]:
        group[0].wait()
    for s in range(2):
        v.csend[4 * s : 4 * s + 4] = v.cf_v[s]
        for j in range(8):
            v.nsend[pl.ds(32 * s + j, 4, stride=8), :] = v.exm_v[s, j]
    for s in range(2):
        for r in range(2):
            for j in range(8):
                for h in range(2):
                    at = 256 * s + (r * 8 + j) * 2 + h
                    v.xsend[pl.ds(at, 8, stride=32), :] = v.exf_v[
                        s, j, r, :, 128 * h : 128 * h + 128
                    ]

    pl.semaphore_wait(barrier, 3 * nr - 1)

    def start_of(owner):
        return jnp.clip(lax.shift_right_logical(owner + 1, 1) - 1, 0, 2)

    def pair_of(owner, s):
        return pl.ds(pl.multiple_of(start_of(owner) * 8 + 32 * s, 8), 16)

    own8 = rows_of(i, 8, 0)
    for d in range(1, nr):
        remote(v.csend, v.crecv.at[1, own8], "c", "c", row_at(d), 0).start()
    for side, dk, rows in ((0, 1, (0, 1, 2)), (2, -1, (5, 6, 7))):
        for to in rows:
            remote(v.csend, v.crecv.at[side, own8], "c", "cs", to, dk).start()

    def send_sample(s):
        for d in range(1, nr):
            remote(
                v.nsend.at[pair_of(row_at(d), s)],
                v.nrecv.at[rows_of(i, 16, 128 * s)],
                "n",
                f"n{s}",
                row_at(d),
                0,
            ).start()
        there = v.nside.at[rows_of(i, 8, 64 * s)]
        remote(v.nsend.at[32 * s + 24 : 32 * s + 32], there, "n", f"ns{s}", 0, 1).start()
        remote(v.nsend.at[32 * s : 32 * s + 8], there, "n", f"ns{s}", 7, -1).start()
        scatter(v.xsend, v.xrecv, "x", f"x{s}", 32, 256 * s)

    send_sample(0)

    row = lax.broadcasted_iota(jnp.int32, (256, 256), 0)
    col = lax.broadcasted_iota(jnp.int32, (256, 256), 1)
    v.gather_m[...] = jnp.where(
        row == 2 * lax.bitwise_and(col, 127) + lax.shift_right_logical(col, 7), F32(1.0), none
    ).astype(BF16)
    for load in loads[3]:
        load.wait()
    pieces = [
        jnp.concatenate(
            [v.em_v[2 * h + e, pl.ds(16 * rl + ca, 8, stride=2), :] for e in range(2)], axis=1
        )
        for rl in range(4)
        for ca in range(2)
        for h in range(2)
    ]
    pieces = permuted(jnp.concatenate(pieces, axis=0), v.gather_m[...])
    for rl in range(4):
        for ca in range(2):
            for h in range(2):
                n = (rl * 2 + ca) * 2 + h
                for cb in range(2):
                    at = h * 16 + rl * 4 + ca * 2 + cb
                    v.esend[pl.ds(at, 8, stride=32), :] = pieces[
                        8 * n : 8 * n + 8, 128 * cb : 128 * cb + 128
                    ]

    scatter(v.esend, v.erecv, "e", "e", 32)
    send_sample(1)

    v.spread_m[...] = jnp.where(
        col == 2 * lax.bitwise_and(row, 127) + lax.shift_right_logical(row, 7), F32(1.0), none
    ).astype(BF16)

    v.crecv[1, own8] = v.csend[...]
    for s in range(2):
        v.nrecv[rows_of(i, 16, 128 * s)] = v.nsend[pair_of(i, s)]
        keep_own(v.xsend, v.xrecv, 32, 256 * s)
    keep_own(v.esend, v.erecv, 32)
    for group in loads[4:]:
        for load in group:
            load.wait()

    entry = lax.broadcasted_iota(jnp.int32, (8, 16), 1)
    place = lax.broadcasted_iota(jnp.int32, (8, 16), 0)
    chosen = []
    for x in range(3):
        index = jnp.zeros((8, 16), jnp.int32)
        for cell in range(8):
            if x == 0:
                number = v.rm_s[cell]
                v.table[x, pl.ds(cell, 8, stride=8), 0:27] = v.km_v[number]
            else:
                number = v.rf_s[2 * cell + x - 1]
                v.table[x, pl.ds(cell, 8, stride=8), 0:27] = v.kf_v[number]
            index = jnp.where(place == cell, number, index)
        chosen.append(jnp.where(index == entry, F32(1.0), none).astype(BF16))
    for x in range(3):
        for c in range(8):
            tile = v.table[x, 8 * c : 8 * c + 8]
            for o in range(27):
                v.kern[x, c, o] = jnp.broadcast_to(tile[:, o : o + 1], (8, 128))
        source = (v.nm_v if x == 0 else v.nf_v)[...].reshape(64, 16)
        high = source.astype(BF16)
        rest = source - high.astype(F32)
        mid = rest.astype(BF16)
        least = (rest - mid.astype(F32)).astype(BF16)
        tile = None
        for piece in (high, mid, least):
            term = lax.dot_general(
                chosen[x], piece, (((1,), (1,)), ((), ())), preferred_element_type=F32
            )
            tile = term if tile is None else tile + term
        for c in range(8):
            for j in range(8):
                at = 8 * c + j
                v.noise[x, c, j] = jnp.broadcast_to(tile[:, at : at + 1], (8, 128))

    for n in range(4):
        for ca in range(2):
            for c in range(4):
                at = pl.ds(16 * n + ca, 8, stride=2)
                lanes = pl.ds(128 * c, 128)
                v.star_x[0, :, 2 * n + ca, lanes] = v.bins_v[c, at, :].astype(F32)
                v.star_x[1, :, 2 * n + ca, lanes] = v.data_v[c, at, :]
    for kind in range(2):
        x = v.star_x[kind, i]
        y = permuted(jnp.concatenate([x[:, :256], x[:, 256:]], axis=0), v.gather_m[...])
        for h in range(2):
            for cb in range(2):
                v.star_y[kind, 2 * h + cb] = y[8 * h : 8 * h + 8, 128 * cb : 128 * cb + 128]
        for h in range(2):
            for cb in range(2):
                for ca in range(2):
                    v.star_z[kind, h, pl.ds(2 * ca + cb, 4, stride=4), :] = v.star_y[
                        kind, 2 * h + cb, pl.ds(ca, 4, stride=2), :
                    ]

    arrived(v.crecv.at[1, 0:56], "c")

    @pl.when((i <= 2) | (i >= 5))
    def _():
        arrived(v.crecv.at[0], "cs")

    for side in range(3):
        for a in range(4):
            for s in range(2):
                x = v.crecv[side, pl.ds(4 * s + a, 8, stride=8), :]
                if side == 0:
                    x = jnp.where(k > 0, x, none)
                if side == 2:
                    x = jnp.where(k < na - 1, x, none)
                v.c12[4 * side + a, s] = x
    base = jnp.where(i > 0, 1, 0) + jnp.where(i == nr - 1, 1, 0)
    spacing = F32(1.0 / (4 * nr))
    cell = 4 * lax.broadcasted_iota(jnp.int32, (8, 256), 0)
    cells = [(cell + j).astype(F32) for j in range(4)]

    def parent_inside(u):
        a = 4 * k + low + u
        return (a >= 0) & (a < 4 * na)

    def star(kind, n, q):
        at = 4 * n + q
        return jnp.concatenate(
            [
                jnp.broadcast_to(v.star_z[kind, h, at : at + 1, :], (8, 128))
                for h in range(2)
            ],
            axis=1,
        )

    def spread_out(sums):
        total = lane_shift(sums[1], 1)
        total = total + lane_shift(sums[0], 2)
        return total + lane_shift(sums[2], 0)

    def forward(s):
        for t in range(4):
            x = v.c12[half_up + 2 + t, s]
            for dr in range(3):
                moved = row_shift(x, dr)
                for db in range(3):
                    v.cs[t, 3 * dr + db] = lane_shift(moved, db)
        arrived(v.nrecv.at[0:112], f"n{s}")

        @pl.when((i == 0) | (i == nr - 1))
        def _():
            arrived(v.nside.at[0:64], f"ns{s}")

        for j in range(8):
            for n in range(2):
                v.emx[1 + n, j] = v.nrecv[pl.ds(128 * s + 8 * n + j, 8, stride=16), :]
            x = v.nside[pl.ds(64 * s + j, 8, stride=8), :]
            v.emx[0, j] = x
            v.emx[3, j] = x
        sums = [[None] * 8, [None] * 8]
        for j in range(8):
            x = [v.emx[base + u, j] for u in range(2)]
            for c in range(8):
                weight = v.noise[0, c, j]
                for u in range(2):
                    term = weight * x[u]
                    sums[u][c] = term if j == 0 else sums[u][c] + term
        for o in range(27):
            dr, da, db = o // 9, o // 3 % 3, o % 3
            x = [v.cs[u + da, 3 * dr + db] for u in range(2)]
            for c in range(8):
                weight = v.kern[0, c, o]
                for u in range(2):
                    sums[u][c] = sums[u][c] + weight * x[u]
        for u in range(2):
            for c in range(8):
                lanes = slice(128 * (c % 2), 128 * (c % 2) + 128)
                v.xi[2 * u + c // 2 % 2, c // 4, :, lanes] = jnp.where(
                    parent_inside(u), sums[u][c], none
                )
        v.m4[...] = permuted(v.xi[...].reshape(64, 256), v.spread_m[...]).reshape(4, 2, 8, 256)
        for da in range(3):
            even = v.m4[first + da, 0]
            odd = v.m4[first + da, 1]
            for m, x in enumerate((row_shift(odd, 0), even, odd, row_shift(even, 2))):
                for db in range(3):
                    v.fs[m, 3 * da + db] = lane_shift(x, db)

        arrived(v.xrecv.at[0:224], f"x{s}")
        for r in range(2):
            sums = [None] * 8
            for j in range(8):
                at = 256 * s + (r * 8 + j) * 2
                x = jnp.concatenate(
                    [v.xrecv[pl.ds(at + h, 8, stride=32), :] for h in range(2)], axis=1
                )
                for c in range(8):
                    term = wide(v.noise[1 + r, c, j]) * x
                    sums[c] = term if j == 0 else sums[c] + term
            for o in range(27):
                x = v.fs[r + o // 9, o % 9]
                for c in range(8):
                    sums[c] = sums[c] + wide(v.kern[1 + r, c, o]) * x
            for c in range(8):
                v.dv[2 * r + c // 4, c % 4] = jnp.exp(sums[c])

    def along(s):
        for q in range(4):
            bins = [star(0, n, q) for n in range(4)]
            light = [
                spacing
                * jnp.concatenate(
                    [v.erecv[pl.ds(16 * h + 4 * j + q, 8, stride=32), :] for h in range(2)], axis=1
                )
                for j in range(4)
            ]
            dens = [v.dv[j, q] for j in range(4)]
            layer = [spacing * x for x in dens]
            depth = sums_before((layer[0] + layer[1]) + (layer[2] + layer[3]))
            shine = []
            for j in range(4):
                shine.append(light[j] * jnp.exp(-depth))
                depth = depth + layer[j]
            column = sums_before((shine[0] + shine[1]) + (shine[2] + shine[3]))
            columns = []
            for j in range(4):
                column = column + shine[j]
                columns.append(column)
            weights = [None] * 4
            for n in range(4):
                picked = jnp.where(bins[n] == cells[0], columns[0], none)
                for j in range(1, 4):
                    picked = jnp.where(bins[n] == cells[j], columns[j], picked)
                picked = row_total(picked)
                left = star(1, n, q) - picked
                for h in range(2):
                    at = 4 * n + q
                    v.res_x[h, at : at + 1] = left[0:1, 128 * h : 128 * h + 128]
                for j in range(4):
                    term = jnp.where(bins[n] > cells[j], left * (picked - columns[j]), none)
                    weights[j] = term if n == 0 else weights[j] + term
            for j in range(4):
                v.dv[j, q] = -dens[j] * weights[j]

        pieces = [
            jnp.concatenate([v.res_x[h, pl.ds(cb, 8, stride=2), :] for cb in range(2)], axis=1)
            for h in range(2)
        ]
        spread = permuted(jnp.concatenate(pieces, axis=0), v.spread_m[...])
        for h in range(2):
            for e in range(2):
                at = 32 * s + 8 * (2 * h + e)
                v.rsend[at : at + 8] = spread[8 * h : 8 * h + 8, 128 * e : 128 * e + 128]
        mine = v.rsend.at[32 * s : 32 * s + 32]
        there = rows_of(i, 32, 256 * s)
        for d in range(1, nr):
            remote(mine, v.rrecv.at[there], "r", f"r{s}", row_at(d), 0).start()
        v.rrecv[there] = mine[...]

    def backward(s):
        for r in range(2):
            grads = [v.dv[2 * r + c // 4, c % 4] for c in range(8)]
            for j in range(8):
                total = weighted([wide(v.noise[1 + r, c, j]) for c in range(8)], grads)
                for h in range(2):
                    at = 256 * s + (2 * j + r) * 2 + h
                    v.gfsend[pl.ds(at, 8, stride=32), :] = total[:, 128 * h : 128 * h + 128]
            for o in range(27):
                total = weighted([wide(v.kern[1 + r, c, o]) for c in range(8)], grads)
                m = r + o // 9
                if r == 1 and m < 3:
                    total = total + v.ws[m, o % 9]
                v.ws[m, o % 9] = total
        scatter(v.gfsend, v.gfrecv, "f", f"f{s}", 32, 256 * s)
        keep_own(v.gfsend, v.gfrecv, 32, 256 * s)

        pieces = []
        for da in range(3):
            moved = [spread_out([v.ws[m, 3 * da + db] for db in range(3)]) for m in range(4)]
            pieces.append(moved[1] + row_shift(moved[3], 0))
            pieces.append(moved[2] + row_shift(moved[0], 2))
        spread = permuted(jnp.concatenate(pieces, axis=0), v.gather_m[...])
        v.h4[...] = jnp.zeros(v.h4.shape, F32)
        for da in range(3):
            keep = parent_inside(lax.shift_right_logical(first + da, 1))
            for cr in range(2):
                n = (2 * da + cr) * 8
                v.h4[first + da, cr] = jnp.where(keep, spread[n : n + 8], none)

        children = []
        for u in range(2):
            children.append([])
            for c in range(8):
                lanes = slice(128 * (c % 2), 128 * (c % 2) + 128)
                children[u].append(v.h4[2 * u + c // 2 % 2, c // 4, :, lanes])
        size = 16 + 8 * s
        for j in range(8):
            weights = [v.noise[0, c, j] for c in range(8)]
            for u in range(2):
                v.hsend[pl.ds(128 * s + 8 * u + j, 8, stride=size), :] = weighted(
                    weights, children[u]
                )
        for dr in range(3):
            for db in range(3):
                sums = [None] * 4
                for da in range(3):
                    o = 9 * dr + 3 * da + db
                    weights = [v.kern[0, c, o] for c in range(8)]
                    for u in range(2):
                        total = weighted(weights, children[u])
                        t = u + da
                        sums[t] = total if sums[t] is None else sums[t] + total
                for t in range(4):
                    v.wq[t, 3 * dr + db] = sums[t]
        v.g12[...] = jnp.zeros(v.g12.shape, F32)
        for t in range(4):
            total = None
            for dr in range(3):
                term = spread_out([v.wq[t, 3 * dr + db] for db in range(3)])
                term = row_shift(term, 2 - dr)
                total = term if total is None else total + term
            v.g12[half_up + 2 + t] = total
        for a in range(4):
            v.hsend[pl.ds(128 + 16 + 4 * s + a, 8, stride=24), :] = v.g12[4 + a]
            for side in range(2):
                outside = (k > 0) if side == 0 else (k < na - 1)
                v.hedge[side, pl.ds(4 * s + a, 8, stride=8), :] = jnp.where(
                    outside, v.g12[8 * side + a], none
                )
        scatter(v.hsend, v.hrecv, "h", f"h{s}", size, 128 * s)
        keep_own(v.hsend, v.hrecv, size, 128 * s)
        for side, dk in ((0, -1), (1, 1)):

            @pl.when(i == 0 if side == 0 else i == nr - 1)
            def _():
                for n in range(nr):
                    at = 128 * s + size * n + 8 * side
                    remote(
                        v.hsend.at[at : at + 8], v.hside.at[side, s], "hs", "hs", n, dk
                    ).start()

    for s in range(2):
        forward(s)
        if s == 0:
            arrived(v.erecv.at[0:224], "e")
        along(s)
        backward(s)
    for side, dk in ((0, -1), (1, 1)):

        @pl.when(i <= 2 if side == 0 else i >= 5)
        def _():
            place = i if side == 0 else i - 2
            for n in range(nr):
                remote(
                    v.hedge.at[side, pl.ds(8 * n, 8)], v.gside.at[place], "gs", "gs", n, dk
                ).start()

    for s in range(2):
        arrived(v.rrecv.at[0:224], f"r{s}")
        for c in range(4):
            for n in range(4):
                for ca in range(2):
                    at = 256 * s + 8 * c + 2 * n + ca
                    v.res_v[c, pl.ds((s * 4 + n) * 16 + ca, 8, stride=2), :] = v.rrecv[
                        pl.ds(at, 8, stride=32), :
                    ]
        arrived(v.gfrecv.at[0:224], f"f{s}")
        for j in range(8):
            for r in range(2):
                for h in range(2):
                    at = 256 * s + (2 * j + r) * 2 + h
                    v.gf_v[s, j, r, :, 128 * h : 128 * h + 128] = v.gfrecv[
                        pl.ds(at, 8, stride=32), :
                    ]
    arrived(v.hrecv.at[0:112], "h0")
    arrived(v.hrecv.at[0:168], "h1")
    arrived(v.gside, "gs")
    arrived(v.hside, "hs")
    for s in range(2):

        def owed(owner, u):
            at = 128 * s + (16 + 8 * s) * owner + 8 * u
            return v.hrecv[at : at + 8]

        by_row = [
            owed(1, 0) + owed(2, 0) + owed(0, 1) + v.hside[1, s],
            owed(3, 0) + owed(4, 0) + owed(1, 1) + owed(2, 1),
            owed(5, 0) + owed(6, 0) + owed(3, 1) + owed(4, 1),
            owed(7, 0) + owed(5, 1) + owed(6, 1) + v.hside[0, s],
        ]
        for a in range(4):
            v.gm_x[pl.ds(32 * s + a, 8, stride=4), :] = by_row[a]
        for j in range(8):
            at = 32 * s + 4 * j
            v.gm_v[s, j] = v.gm_x[at : at + 4]
    total = v.gside[0]
    for n in range(1, 6):
        total = total + v.gside[n]
    for owner in range(nr):
        at = 128 + 24 * owner + 16
        total = total + v.hrecv[at : at + 8]
    for s in range(2):
        v.gc_v[s] = total[4 * s : 4 * s + 4]

    sent(v.xsend.at[0:104], "c")
    sent(v.xsend.at[0:256], "n")
    sent(v.xsend.at[0:448], "x")
    sent(v.xsend.at[0:224], "e")
    sent(v.xsend.at[0:448], "r")
    sent(v.xsend.at[0:448], "f")
    sent(v.xsend.at[0:280], "h")

    @pl.when((i <= 2) | (i >= 5))
    def _():
        sent(v.xsend.at[0:64], "gs")

    @pl.when((i == 0) | (i == nr - 1))
    def _():
        sent(v.xsend.at[0:128], "hs")


def hand_out(gc_v, gm_v, gf_v, res_v, gc_o, gm_o, gf_o, res_o, sem):
    outs = [
        pltpu.make_async_copy(gf_v, gf_o, sem.at[0]),
        pltpu.make_async_copy(gm_v, gm_o.at[:, :, 0], sem.at[1]),
        pltpu.make_async_copy(gc_v, gc_o.at[:, 0], sem.at[2]),
    ]
    for c in range(4):
        outs.append(
            pltpu.make_async_copy(
                res_v.at[c].reshape(2, 4, 16, 128),
                res_o.at[:, :, :, pl.ds(128 * c, 128)],
                sem.at[3 + c],
            )
        )
    for out in outs:
        out.start()
    for out in outs:
        out.wait()


def per_device(*args):
    nr, na = lax.axis_size("rad"), lax.axis_size("ang")
    args = list(args)
    for n in (4, 7):
        args[n] = args[n].transpose(1, 2, 0)
    held = [(2, 4, 128), (2, 8, 4, 128), (2, 8, 2, 8, 256), (4, 128, 128)]
    shapes = [(2, 1, 4, 128), (2, 8, 1, 4, 128), (2, 8, 2, 8, 256), (2, 4, 16, 512)]
    results = pl.pallas_call(
        functools.partial(kernel, nr, na),
        out_shape=[pltpu.VMEM(shape, F32) for shape in held],
        in_specs=[ANY] * 12,
        out_specs=[VMEM] * 4,
        scratch_shapes=list(SCRATCH.values()),
        compiler_params=pltpu.CompilerParams(collective_id=0, has_side_effects=True),
    )(*args)
    return pl.pallas_call(
        hand_out,
        out_shape=[jax.ShapeDtypeStruct(shape, F32) for shape in shapes],
        in_specs=[VMEM] * 4,
        out_specs=[ANY] * 4,
        scratch_shapes=[pltpu.SemaphoreType.DMA((7,))],
        compiler_params=pltpu.CompilerParams(vmem_limit_bytes=4 << 20),
    )(*results)


def solution(mesh):
    placed = (
        P(None, "rad", "ang", None),
        P(None, None, "rad", "ang", None),
        P(None, None, "rad", "ang", None),
        P(),
        P(),
        P(),
        P(),
        P(),
        P(),
        P("rad", "ang", None),
        P(None, "ang", None),
        P(None, "ang", None),
    )
    return jax.shard_map(
        per_device,
        mesh=mesh,
        in_specs=placed,
        out_specs=(
            P(None, "rad", "ang", None),
            P(None, None, "rad", "ang", None),
            P(None, None, "rad", "ang", None),
            P(None, None, "ang", None),
        ),
        check_vma=False,
    )
```

time: 32.5 us -> 30.4 us (0.935)
  the two profiles are of different devices: /device:TPU:3 before, /device:TPU:1 now
where the time goes in v2:
time: 30.4 us; the launch traced here: 30.3 us
  Pallas kernels  29.6 us (97%)
  between operations  0.64 us (2%)
    pallas_call x1, Pallas kernels, per_device(): pl.pallas_call(functools.partial(kernel, nr, na), out_shape=[pltpu.VMEM(s...  28.8 us
    pallas_call x1, Pallas kernels, per_device(): pl.pallas_call(hand_out, out_shape=[jax.ShapeDtypeStruct(shape, F32) for...  0.86 us

profile of v2, /device:TPU:1, one launch (start us, length us, event | category | flops | bytes accessed | tf_op | source)
XLA Modules:
  0.0 30.3 jit_solution(16338209617533992834)
XLA Ops:
  0.6 28.8 %shard_map.147 = (f32[2,4,128]{2,1,0:T(4,128)S(1)}, f32[2,8,4,128]{3,2,1,0:T(4,128)S(1)}, f32[2,8,2,8,256]{4,3,2,1,0:T(8,128)S(1)}, f32[4,128,128]{2,1,0:T(8,128)S(1)}) custom-call(f32[2,1,4,128]{3,2,1,0:T(4,128)} %refs_0_.1, f32[2,8,1,4,128]{4,3,2,1,0:T(4,128)} %refs_1_.1, f32[2,8,2,8,256]{4,3,2,1,0:T(8,128)} %refs_2_.1, f32[16,8,27]{2,1,0:T(8,128)} %refs_3_.1, ...), custom_call_target="tpu_custom_call" | custom-call | tf_op jit(solution)/shard_map/pallas_call | solution.py:730
  29.4 0.9 %shard_map.148 = (f32[2,1,4,128]{3,2,1,0:T(4,128)}, f32[2,8,1,4,128]{4,3,2,1,0:T(4,128)}, f32[2,8,2,8,256]{4,3,2,1,0:T(8,128)}, f32[2,4,16,512]{3,2,1,0:T(8,128)}) custom-call(f32[2,4,128]{2,1,0:T(4,128)S(1)} %get-tuple-element.8.gc_v, f32[2,8,4,128]{3,2,1,0:T(4,128)S(1)} %get-tuple-element.9.gm_v, f32[2,8,2,8,256]{4,3,2,1,0:T(8,128)S(1)} %get-tuple-element.10.gf_v, ...), custom_call_target="tpu_custom_call" | custom-call | tf_op jit(solution)/shard_map/pallas_call | solution.py:738

commit v3 on v2

--- a/solution.py
+++ b/solution.py
@@ -88,16 +88,16 @@
     hside=pltpu.VMEM((2, 2, 8, 128), F32),
     gside=pltpu.VMEM((6, 8, 128), F32),
     gm_x=pltpu.VMEM((64, 128), F32),
-    load_sem=pltpu.SemaphoreType.DMA((12,)),
+    load_sem=pltpu.SemaphoreType.DMA((13,)),
     send_sem=pltpu.SemaphoreType.DMA((9,)),
-    recv_sem=pltpu.SemaphoreType.DMA((17,)),
+    recv_sem=pltpu.SemaphoreType.DMA((19,)),
 )
 SEND = dict(c=0, n=1, x=2, e=3, r=4, f=5, h=6, gs=7, hs=8)
 RECV = {
     name: number
     for number, name in enumerate(
         ["c", "cs", "n0", "n1", "ns0", "ns1", "x0", "x1", "e"]
-        + ["r0", "r1", "f0", "f1", "h0", "h1", "gs", "hs"]
+        + ["r0", "r1", "q0", "q1", "f0", "f1", "h0", "h1", "gs", "hs"]
     )
 }
 INPUTS = ["cf", "exm", "exf", "km", "nm", "rm", "kf", "nf", "rf", "emi", "bins", "data"]
@@ -197,9 +197,12 @@
         dst[own] = src[own]
 
     loads = [
-        [pltpu.make_async_copy(v.exf, v.exf_v, v.load_sem.at[0])],
+        [pltpu.make_async_copy(v.cf.at[:, 0], v.cf_v, v.load_sem.at[2])],
         [pltpu.make_async_copy(v.exm.at[:, :, 0], v.exm_v, v.load_sem.at[1])],
-        [pltpu.make_async_copy(v.cf.at[:, 0], v.cf_v, v.load_sem.at[2])],
+        [
+            pltpu.make_async_copy(v.exf.at[s], v.exf_v.at[s], v.load_sem.at[(0, 12)[s]])
+            for s in range(2)
+        ],
     ]
     for n, (src, dst) in enumerate(((v.emi, v.em_v), (v.bins, v.bins_v), (v.data, v.data_v))):
         loads.append(
@@ -223,7 +226,7 @@
         )
     ):
         loads.append([pltpu.make_async_copy(src, dst, v.load_sem.at[6 + n])])
-    for group in loads:
+    for group in loads[:3]:
         for load in group:
             load.start()
 
@@ -236,21 +239,15 @@
                 barrier, inc=1, device_id=(d, block_at(dk)), device_id_type=MESH
             )
 
-    for group in loads[:3]:
+    for group in loads[3:]:
+        for load in group:
+            load.start()
+    for group in loads[:2]:
         group[0].wait()
     for s in range(2):
         v.csend[4 * s : 4 * s + 4] = v.cf_v[s]
         for j in range(8):
             v.nsend[pl.ds(32 * s + j, 4, stride=8), :] = v.exm_v[s, j]
-    for s in range(2):
-        for r in range(2):
-            for j in range(8):
-                for h in range(2):
-                    at = 256 * s + (r * 8 + j) * 2 + h
-                    v.xsend[pl.ds(at, 8, stride=32), :] = v.exf_v[
-                        s, j, r, :, 128 * h : 128 * h + 128
-                    ]
-
     pl.semaphore_wait(barrier, 3 * nr - 1)
 
     def start_of(owner):
@@ -279,6 +276,14 @@
         there = v.nside.at[rows_of(i, 8, 64 * s)]
         remote(v.nsend.at[32 * s + 24 : 32 * s + 32], there, "n", f"ns{s}", 0, 1).start()
         remote(v.nsend.at[32 * s : 32 * s + 8], there, "n", f"ns{s}", 7, -1).start()
+        loads[2][s].wait()
+        for r in range(2):
+            for j in range(8):
+                for h in range(2):
+                    at = 256 * s + (r * 8 + j) * 2 + h
+                    v.xsend[pl.ds(at, 8, stride=32), :] = v.exf_v[
+                        s, j, r, :, 128 * h : 128 * h + 128
+                    ]
         scatter(v.xsend, v.xrecv, "x", f"x{s}", 32, 256 * s)
 
     send_sample(0)
@@ -534,8 +539,8 @@
                 v.rsend[at : at + 8] = spread[8 * h : 8 * h + 8, 128 * e : 128 * e + 128]
         mine = v.rsend.at[32 * s : 32 * s + 32]
         there = rows_of(i, 32, 256 * s)
-        for d in range(1, nr):
-            remote(mine, v.rrecv.at[there], "r", f"r{s}", row_at(d), 0).start()
+        for to in (ring_at(1), ring_at(3), ring_at(2), across):
+            remote(mine, v.rrecv.at[there], "r", f"r{s}", to, 0).start()
         v.rrecv[there] = mine[...]
 
     def backward(s):
@@ -620,6 +625,18 @@
                         v.hsend.at[at : at + 8], v.hside.at[side, s], "hs", "hs", n, dk
                     ).start()
 
+    def ring_at(d):
+        return (i & 4) + ((i + d) & 3)
+
+    across = i ^ 4
+
+    def pass_on(s):
+        arrived(v.rrecv.at[0:128], f"r{s}")
+        opposite = ring_at(2)
+        for owner, to in ((across, ring_at(1)), (across, ring_at(3)), (opposite, across)):
+            block = v.rrecv.at[rows_of(owner, 32, 256 * s)]
+            remote(block, block, "r", f"q{s}", to, 0).start()
+
     for s in range(2):
         forward(s)
         if s == 0:
@@ -636,8 +653,10 @@
                     v.hedge.at[side, pl.ds(8 * n, 8)], v.gside.at[place], "gs", "gs", n, dk
                 ).start()
 
+    pass_on(0)
+    pass_on(1)
     for s in range(2):
-        arrived(v.rrecv.at[0:224], f"r{s}")
+        arrived(v.rrecv.at[0:96], f"q{s}")
         for c in range(4):
             for n in range(4):
                 for ca in range(2):

time: 30.4 us -> 29.3 us (0.964)
  Pallas kernels: 29.6 us -> 28.5 us
    pallas_call x1, Pallas kernels: 28.8 us -> 27.7 us  [per_device(): pl.pallas_call(functools.partial(kernel, nr, na), out_shape=[pltpu.VMEM(s...]
where the time goes in v3:
time: 29.3 us; the launch traced here: 29.2 us
  Pallas kernels  28.5 us (97%)
  between operations  0.64 us (2%)
    pallas_call x1, Pallas kernels, per_device(): pl.pallas_call(functools.partial(kernel, nr, na), out_shape=[pltpu.VMEM(s...  27.7 us
    pallas_call x1, Pallas kernels, per_device(): pl.pallas_call(hand_out, out_shape=[jax.ShapeDtypeStruct(shape, F32) for...  0.86 us

profile of v3, /device:TPU:1, one launch (start us, length us, event | category | flops | bytes accessed | tf_op | source)
XLA Modules:
  0.0 29.2 jit_solution(16160105640749329822)
XLA Ops:
  0.6 27.7 %shard_map.147 = (f32[2,4,128]{2,1,0:T(4,128)S(1)}, f32[2,8,4,128]{3,2,1,0:T(4,128)S(1)}, f32[2,8,2,8,256]{4,3,2,1,0:T(8,128)S(1)}, f32[4,128,128]{2,1,0:T(8,128)S(1)}) custom-call(f32[2,1,4,128]{3,2,1,0:T(4,128)} %refs_0_.1, f32[2,8,1,4,128]{4,3,2,1,0:T(4,128)} %refs_1_.1, f32[2,8,2,8,256]{4,3,2,1,0:T(8,128)} %refs_2_.1, f32[16,8,27]{2,1,0:T(8,128)} %refs_3_.1, ...), custom_call_target="tpu_custom_call" | custom-call | tf_op jit(solution)/shard_map/pallas_call | solution.py:749
  28.3 0.9 %shard_map.148 = (f32[2,1,4,128]{3,2,1,0:T(4,128)}, f32[2,8,1,4,128]{4,3,2,1,0:T(4,128)}, f32[2,8,2,8,256]{4,3,2,1,0:T(8,128)}, f32[2,4,16,512]{3,2,1,0:T(8,128)}) custom-call(f32[2,4,128]{2,1,0:T(4,128)S(1)} %get-tuple-element.8.gc_v, f32[2,8,4,128]{3,2,1,0:T(4,128)S(1)} %get-tuple-element.9.gm_v, f32[2,8,2,8,256]{4,3,2,1,0:T(8,128)S(1)} %get-tuple-element.10.gf_v, ...), custom_call_target="tpu_custom_call" | custom-call | tf_op jit(solution)/shard_map/pallas_call | solution.py:757

commit v4 on v3

--- a/solution.py
+++ b/solution.py
@@ -182,7 +182,7 @@
         return pl.ds(pl.multiple_of(index * size + offset, 8), size)
 
     def scatter(src, dst, group, arrival, size, offset=0):
-        for d in range(1, nr):
+        for d in (1, 7, 2, 6, 3, 5, 4):
             remote(
                 src.at[rows_of(row_at(d), size, offset)],
                 dst.at[rows_of(i, size, offset)],
@@ -257,14 +257,14 @@
         return pl.ds(pl.multiple_of(start_of(owner) * 8 + 32 * s, 8), 16)
 
     own8 = rows_of(i, 8, 0)
-    for d in range(1, nr):
+    for d in (1, 7, 2, 6, 3, 5, 4):
         remote(v.csend, v.crecv.at[1, own8], "c", "c", row_at(d), 0).start()
     for side, dk, rows in ((0, 1, (0, 1, 2)), (2, -1, (5, 6, 7))):
         for to in rows:
             remote(v.csend, v.crecv.at[side, own8], "c", "cs", to, dk).start()
 
     def send_sample(s):
-        for d in range(1, nr):
+        for d in (1, 7, 2, 6, 3, 5, 4):
             remote(
                 v.nsend.at[pair_of(row_at(d), s)],
                 v.nrecv.at[rows_of(i, 16, 128 * s)],

time: 29.3 us -> 28.9 us (0.986)
  Pallas kernels: 28.5 us -> 28.2 us
    pallas_call x1, Pallas kernels: 27.7 us -> 27.3 us  [per_device(): pl.pallas_call(functools.partial(kernel, nr, na), out_shape=[pltpu.VMEM(s...]
where the time goes in v4:
time: 28.9 us; the launch traced here: 28.8 us
  Pallas kernels  28.2 us (98%)
  between operations  0.64 us (2%)
    pallas_call x1, Pallas kernels, per_device(): pl.pallas_call(functools.partial(kernel, nr, na), out_shape=[pltpu.VMEM(s...  27.3 us
    pallas_call x1, Pallas kernels, per_device(): pl.pallas_call(hand_out, out_shape=[jax.ShapeDtypeStruct(shape, F32) for...  0.86 us

profile of v4, /device:TPU:1, one launch (start us, length us, event | category | flops | bytes accessed | tf_op | source)
XLA Modules:
  0.0 28.8 jit_solution(15287802514813589754)
XLA Ops:
  0.6 27.3 %shard_map.147 = (f32[2,4,128]{2,1,0:T(4,128)S(1)}, f32[2,8,4,128]{3,2,1,0:T(4,128)S(1)}, f32[2,8,2,8,256]{4,3,2,1,0:T(8,128)S(1)}, f32[4,128,128]{2,1,0:T(8,128)S(1)}) custom-call(f32[2,1,4,128]{3,2,1,0:T(4,128)} %refs_0_.1, f32[2,8,1,4,128]{4,3,2,1,0:T(4,128)} %refs_1_.1, f32[2,8,2,8,256]{4,3,2,1,0:T(8,128)} %refs_2_.1, f32[16,8,27]{2,1,0:T(8,128)} %refs_3_.1, ...), custom_call_target="tpu_custom_call" | custom-call | tf_op jit(solution)/shard_map/pallas_call | solution.py:749
  28.0 0.9 %shard_map.148 = (f32[2,1,4,128]{3,2,1,0:T(4,128)}, f32[2,8,1,4,128]{4,3,2,1,0:T(4,128)}, f32[2,8,2,8,256]{4,3,2,1,0:T(8,128)}, f32[2,4,16,512]{3,2,1,0:T(8,128)}) custom-call(f32[2,4,128]{2,1,0:T(4,128)S(1)} %get-tuple-element.8.gc_v, f32[2,8,4,128]{3,2,1,0:T(4,128)S(1)} %get-tuple-element.9.gm_v, f32[2,8,2,8,256]{4,3,2,1,0:T(8,128)S(1)} %get-tuple-element.10.gf_v, ...), custom_call_target="tpu_custom_call" | custom-call | tf_op jit(solution)/shard_map/pallas_call | solution.py:757
